TPU v7x, 256 devices: a whole 4x4x8 slice. The times are simulated.
256 devices in a mesh: sel: 64 (over y, z, core), mdl: 4 (over x).
Axes of the slice: x: 4, y: 4, z: 8, core: 2. Of those that a mesh axis runs over, the one named last changes fastest.
Arguments:
- patches: bfloat16 [49152, 1408], P('sel', 'mdl'), may hold values from -6 to 6
- text: bfloat16 [8192, 1024], P('sel', 'mdl'), may hold values from -64 to 64
- ref_proj: bfloat16 [1408, 1024], P(None, 'mdl'), may hold values from -0.15625 to 0.15625
- w_up: bfloat16 [1408, 6144], P(None, 'mdl'), may hold values from -0.15625 to 0.15625
- w_down: bfloat16 [6144, 1408], P('mdl'), may hold values from -0.078125 to 0.078125
- kept_index: int32 [4096], P('sel'), may hold values from 0 to 127, as said below
- dest: int32 [4096], P('sel'), may hold values from 0 to 63, as said below
- cotan: bfloat16 [24576, 1408], P('sel', 'mdl'), may hold values from -16 to 16
Outputs:
- ref_loss: float32 [8192], P('sel')
- learnability: float32 [4096], P('sel')
- grad_up: float32 [1408, 6144], P('sel', 'mdl')
Inputs may be any that keep to these rules, and one draw needn't show every extreme that they name: `kept_index`: the 64 entries of one scorer shard are distinct. `dest`: on each scorer shard at most 2 kept entries name the same learner shard; one learner shard is named by exactly 2 kept entries of every scorer shard.
All inputs are finite; a program needn't handle non-finite values.
Results may differ from a plain program's by a relative error of at most 0.019.
Values may be sent and summed in bfloat16 or wider, within the bound.
A program may use at most 128 MiB of HBM per device.

v0:
```python
import jax
import jax.numpy as jnp
from jax import lax
from jax.sharding import PartitionSpec as P

logit_scale = 64.0
eps = 1e-06


def gelu_parts(pre_act):
    cumul = 0.5 * (1.0 + lax.erf(pre_act * 0.7071067811865476))
    density = jnp.exp(-0.5 * pre_act * pre_act) * 0.3989422804014327
    return (pre_act * cumul, cumul + pre_act * density)


def partial_scores(rows_hat, text_all):
    return lax.dot_general(
        rows_hat, text_all, (((1,), (1,)), ((), ())), preferred_element_type=jnp.float32
    )


def exp_total(rows_full, text_share):
    return jnp.sum(jnp.exp(logit_scale * partial_scores(rows_full, text_share)), axis=1)


def own_product(rows_part, texts_part):
    return jnp.sum(rows_part.astype(jnp.float32) * texts_part.astype(jnp.float32), axis=1)


def learn(kept_tok, kept_cot, row_weight, w_up, w_down, ref_proj):
    n_items, n_patch, d_part = kept_tok.shape
    n_rows = n_items * n_patch
    weighted = (kept_cot.astype(jnp.float32) * row_weight[:, None, None]).astype(jnp.bfloat16)
    tok_full, cot_full = (
        lax.all_gather(kept_tok.reshape(n_rows, d_part), "mdl", axis=1, tiled=True),
        lax.all_gather(weighted.reshape(n_rows, d_part), "mdl", axis=1, tiled=True),
    )
    pre_act = jnp.dot(tok_full, w_up, preferred_element_type=jnp.float32)
    activated, gelu_slope = gelu_parts(pre_act)
    hidden = activated.astype(jnp.bfloat16)
    mixed_part = jnp.dot(hidden, w_down, preferred_element_type=jnp.float32)
    summed = lax.psum_scatter(mixed_part, "mdl", scatter_dimension=1, tiled=True)
    outputs = summed + kept_tok.reshape(n_rows, d_part).astype(jnp.float32)
    pooled = jnp.mean(outputs.reshape(n_items, n_patch, d_part), axis=1).astype(jnp.bfloat16)
    pooled_full = lax.all_gather(pooled, "mdl", axis=1, tiled=True)
    learn_emb = jnp.dot(pooled_full, ref_proj, preferred_element_type=jnp.float32)
    learn_sq = lax.psum(jnp.sum(learn_emb * learn_emb, axis=1), "mdl")
    learn_hat = (learn_emb * lax.rsqrt(learn_sq + eps)[:, None]).astype(jnp.bfloat16)
    grad_act = lax.dot_general(
        cot_full, w_down, (((1,), (1,)), ((), ())), preferred_element_type=jnp.float32
    )
    grad_pre = (grad_act * gelu_slope).astype(jnp.bfloat16)
    grad_up = lax.psum_scatter(
        lax.dot_general(
            tok_full, grad_pre, (((0,), (0,)), ((), ())), preferred_element_type=jnp.float32
        ),
        "sel",
        scatter_dimension=0,
        tiled=True,
    )
    return (learn_hat, grad_up)


def per_device(patches, text, ref_proj, w_up, w_down, kept_index, dest, cotan):
    n_sel = lax.axis_size("sel")
    ex_dev = text.shape[0]
    d_part = patches.shape[1]
    n_patch = patches.shape[0] // ex_dev
    k_dev = kept_index.shape[0]
    blocks = patches.reshape(ex_dev, n_patch, d_part)
    pooled = jnp.mean(blocks, axis=1, dtype=jnp.float32).astype(jnp.bfloat16)
    pooled_full = lax.all_gather(pooled, "mdl", axis=1, tiled=True)
    img_emb = jnp.dot(pooled_full, ref_proj, preferred_element_type=jnp.float32)
    text_vals = text.astype(jnp.float32)
    img_sq, text_sq = lax.psum(
        (jnp.sum(img_emb * img_emb, axis=1), jnp.sum(text_vals * text_vals, axis=1)), "mdl"
    )
    img_hat = (img_emb * lax.rsqrt(img_sq + eps)[:, None]).astype(jnp.bfloat16)
    text_hat = (text_vals * lax.rsqrt(text_sq + eps)[:, None]).astype(jnp.bfloat16)
    text_rows = lax.all_to_all(text_hat, "mdl", split_axis=0, concat_axis=1, tiled=True)
    text_split = lax.all_gather(text_rows, "sel", axis=0, tiled=True)
    img_full = lax.all_gather(img_hat, "mdl", axis=1, tiled=True)
    ref_total, ref_own = lax.psum(
        (exp_total(img_full, text_split), own_product(img_hat, text_hat)), "mdl"
    )
    ref_loss = jnp.log(ref_total) - logit_scale * ref_own
    kept_tok = blocks[kept_index]
    kept_cot = cotan.reshape(k_dev, n_patch, d_part)
    onehot = (dest[:, None] == jnp.arange(n_sel, dtype=jnp.int32)[None, :]).astype(jnp.int32)
    capacity = 2 * k_dev // n_sel
    dest_rank = jnp.sum(jnp.cumsum(onehot, axis=0) * onehot, axis=1) - 1
    slot_idx = dest * capacity + dest_rank
    inverse = (
        jnp.full((n_sel * capacity,), k_dev, jnp.int32)
        .at[slot_idx]
        .set(jnp.arange(k_dev, dtype=jnp.int32))
    )
    live_flag = (inverse < k_dev).astype(jnp.int32)
    pad_tok = jnp.concatenate([kept_tok, jnp.zeros((1, n_patch, d_part), jnp.bfloat16)], axis=0)[
        inverse
    ]
    pad_cot = jnp.concatenate([kept_cot, jnp.zeros((1, n_patch, d_part), jnp.bfloat16)], axis=0)[
        inverse
    ]
    recv_tok, recv_cot, recv_live = (
        lax.all_to_all(pad_tok, "sel", split_axis=0, concat_axis=0, tiled=True),
        lax.all_to_all(pad_cot, "sel", split_axis=0, concat_axis=0, tiled=True),
        lax.all_to_all(live_flag, "sel", split_axis=0, concat_axis=0, tiled=True),
    )
    learn_count = jnp.maximum(jnp.sum(recv_live), 1).astype(jnp.float32)
    row_weight = recv_live.astype(jnp.float32) / learn_count
    slot_hat, grad_up = learn(recv_tok, recv_cot, row_weight, w_up, w_down, ref_proj)
    returned = lax.all_to_all(slot_hat, "sel", split_axis=0, concat_axis=0, tiled=True)
    kept_hat = returned[slot_idx]
    learn_full = lax.all_gather(kept_hat, "mdl", axis=1, tiled=True)
    learn_total, learn_own = lax.psum(
        (exp_total(learn_full, text_split), own_product(kept_hat, text_hat[kept_index])), "mdl"
    )
    learner_loss = jnp.log(learn_total) - logit_scale * learn_own
    learnability = learner_loss - ref_loss[kept_index]
    return (ref_loss, learnability, grad_up)


def solution(mesh):
    in_specs = (
        P("sel", "mdl"),
        P("sel", "mdl"),
        P(None, "mdl"),
        P(None, "mdl"),
        P("mdl", None),
        P("sel"),
        P("sel"),
        P("sel", "mdl"),
    )
    out_specs = (P("sel"), P("sel"), P("sel", "mdl"))
    return jax.shard_map(
        per_device, mesh=mesh, in_specs=in_specs, out_specs=out_specs, check_vma=False
    )
```

profile of v0, /device:TPU:25, one launch (start us, length us, event | category | flops | bytes accessed | tf_op | source)
XLA Modules:
  0.0 445.0 jit_solution(873376616662270338)
XLA Ops:
  14.2 35.0 %all_to_all.55 = bf16[128,6,352]{2,1,0:T(8,128)(2,1)S(1)} all-to-all(bf16[128,6,352]{2,1,0:T(8,128)(2,1)S(1)} %gather_fusion.1), channel_id=1, replica_groups=mesh['sel'=64,'mdl'=4] {'sel'}, dimensions={0} | all-to-all | bytes 1081344 | tf_op jit(solution)/shard_map/all_to_all | solution.py:106
  50.7 30.7 %all-gather.7.cloned.1.call-done = bf16[768,1408]{0,1:T(8,128)(2,1)} async-done(((bf16[768,352]{0,1:T(8,128)(2,1)}), bf16[768,1408]{0,1:T(8,128)(2,1)}) %all-gather.7.cloned.1.call-update) | async-done | bytes 2162704 | tf_op jit(solution)/shard_map/all_gather | solution.py:35
  81.4 6.4 %fusion.18 = f32[768,1536]{1,0:T(8,128)S(1)} fusion(bf16[768,1408]{0,1:T(8,128)(2,1)} %all-gather.7.cloned.1.call-done, bf16[1408,1536]{1,0:T(8,128)(2,1)} %param.11), kind=kOutput, calls=%fused_computation.57 | convolution fusion | flops 3321888768 | bytes 11206656 | tf_op jit(solution)/shard_map/dot_general | solution.py:38
  90.0 9.1 %fusion.8 = f32[768,1408]{0,1:T(8,128)} fusion(bf16[1536,1408]{1,0:T(8,128)(2,1)} %param.12, f32[768,1536]{1,0:T(8,128)S(1)} %fusion.18), kind=kOutput, calls=%fused_computation.18 | convolution fusion | flops 3327787008 | bytes 13369344 | tf_op jit(solution)/shard_map/dot_general | solution.py:41
  99.9 11.0 %all-to-all-start.4 = ((s32[64,2,1]{1,2,0:T(1,128)}), s32[64,2,1]{1,2,0:T(1,128)S(1)}, u32[]{:S(2)}, u32[]{:S(2)}) async-start(s32[64,2,1]{1,2,0:T(1,128)} %bitcast.2), calls=%async_computation.5 | async-start | bytes 65536 | tf_op jit(solution)/shard_map/all_to_all | solution.py:108
  113.0 5.1 %all-to-all-done.4 = s32[64,2,1]{1,2,0:T(1,128)S(1)} async-done(((s32[64,2,1]{1,2,0:T(1,128)}), s32[64,2,1]{1,2,0:T(1,128)S(1)}, u32[]{:S(2)}, u32[]{:S(2)}) %all-to-all-start.4) | async-done | bytes 544 | tf_op jit(solution)/shard_map/all_to_all | solution.py:108
  118.2 6.9 %all-to-all-start.3 = ((bf16[128,6,352]{2,1,0:T(8,128)(2,1)}), bf16[128,6,352]{2,1,0:T(8,128)(2,1)S(1)}, u32[]{:S(2)}, u32[]{:S(2)}) async-start(bf16[128,6,352]{2,1,0:T(8,128)(2,1)} %gather_fusion.5), calls=%async_computation.4 | async-start | bytes 1572864 | tf_op jit(solution)/shard_map/all_to_all | solution.py:107
  126.7 21.1 %all-to-all-done.3 = bf16[128,6,352]{2,1,0:T(8,128)(2,1)S(1)} async-done(((bf16[128,6,352]{2,1,0:T(8,128)(2,1)}), bf16[128,6,352]{2,1,0:T(8,128)(2,1)S(1)}, u32[]{:S(2)}, u32[]{:S(2)}) %all-to-all-start.3) | async-done | bytes 540704 | tf_op jit(solution)/shard_map/all_to_all | solution.py:107
  152.4 10.9 %all_gather.21 = bf16[128,1408]{0,1:T(8,128)(2,1)S(1)} all-gather(bf16[128,352]{0,1:T(8,128)(2,1)S(1)} %multiply_convert_fusion.4), channel_id=1, replica_groups=mesh['sel'=64,'mdl'=4] {'mdl'}, dimensions={1}, use_global_device_ids=true | all-gather | bytes 450560 | tf_op jit(solution)/shard_map/all_gather | solution.py:72
  168.9 12.2 %all_gather.25 = bf16[128,1408]{0,1:T(8,128)(2,1)S(1)} all-gather(bf16[128,352]{0,1:T(8,128)(2,1)S(1)} %multiply_convert_fusion.3), channel_id=1, replica_groups=mesh['sel'=64,'mdl'=4] {'mdl'}, dimensions={1}, use_global_device_ids=true | all-gather | bytes 450560 | tf_op jit(solution)/shard_map/all_gather | solution.py:45
  181.5 7.6 %all-reduce.5 = (f32[128]{0:T(128)S(1)}, f32[128]{0:T(128)S(1)}, f32[128]{0:T(128)S(1)}) all-reduce(f32[128]{0:T(128)S(1)} %fusion.12, f32[128]{0:T(128)S(1)} %get-tuple-element.13, f32[128]{0:T(128)S(1)} %get-tuple-element.15), channel_id=1, replica_groups=mesh['sel'=64,'mdl'=4] {'mdl'}, use_global_device_ids=true, to_apply=%region_4.0 | all-reduce | flops 384 | bytes 3072 | tf_op jit(solution)/shard_map/psum | solution.py:75
  190.3 6.8 %all_to_all.56 = bf16[4,32,256]{2,1,0:T(8,128)(2,1)S(1)} all-to-all(bf16[4,32,256]{2,1,0:T(8,128)(2,1)S(1)} %bitcast.31), channel_id=1, replica_groups=mesh['sel'=64,'mdl'=4] {'mdl'}, dimensions={0} | all-to-all | bytes 131072 | tf_op jit(solution)/shard_map/all_to_all | solution.py:80
  197.8 13.5 %fusion.19 = f32[1408,1536]{1,0:T(8,128)} fusion(bf16[768,1408]{0,1:T(8,128)(2,1)} %all-gather.7.cloned.1.call-done, f32[768,1536]{1,0:T(8,128)} %copy-done.7, bf16[768,1408]{0,1:T(8,128)(2,1)} %all-gather.9.cloned.1.call-done, bf16[1536,1408]{1,0:T(8,128)(2,1)} %param.12), kind=kOutput, calls=%fused_computation.58 | convolution fusion | flops 6655574016 | bytes 22020096 | tf_op jit(solution)/shard_map/dot_general | solution.py:54
  211.3 135.2 %fusion = f32[24,1536]{1,0:T(8,128)S(1)} fusion(f32[1408,1536]{1,0:T(8,128)} %fusion.19), kind=kCustom, calls=%all-reduce-scatter | all-reduce-scatter fusion | flops 2359297 | bytes 8799232
  346.4 3.8 collective-permute-start.5
  350.3 15.4 %collective-permute-start.4 = (f32[24,1536]{1,0:T(8,128)S(1)}, f32[24,1536]{1,0:T(8,128)S(1)}, u32[]{:S(2)}, u32[]{:S(2)}) collective-permute-start(f32[24,1536]{1,0:T(8,128)S(1)} %fusion), channel_id=1, source_target_pairs={{0,20},{4,24},{8,28},{12,32},{16,36},{20,40},{24,44},{28,48},{32,5... | collective-permute-start | bytes 442376
  367.7 11.0 %collective-permute-start.2 = (f32[24,1536]{1,0:T(8,128)S(1)}, f32[24,1536]{1,0:T(8,128)S(1)}, u32[]{:S(2)}, u32[]{:S(2)}) collective-permute-start(f32[24,1536]{1,0:T(8,128)S(1)} %fusion), channel_id=1, source_target_pairs={{0,12},{4,16},{8,20},{12,24},{16,28},{20,32},{24,36},{28,40},{32,4... | collective-permute-start | bytes 442376
  380.6 2.5 collective-permute-start
  384.3 5.2 %collective-permute-done.1 = f32[24,1536]{1,0:T(8,128)S(1)} collective-permute-done((f32[24,1536]{1,0:T(8,128)S(1)}, f32[24,1536]{1,0:T(8,128)S(1)}, u32[]{:S(2)}, u32[]{:S(2)}) %collective-permute-start.1) | collective-permute-done | bytes 147488
  391.4 11.5 %all-to-all-start.2 = ((bf16[64,2,256]{2,1,0:T(2,128)(2,1)}), bf16[64,2,256]{2,1,0:T(2,128)(2,1)S(1)}, u32[]{:S(2)}, u32[]{:S(2)}) async-start(bf16[64,2,256]{2,1,0:T(2,128)(2,1)} %all_to_all.41), calls=%async_computation.3 | async-start | bytes 131072 | tf_op jit(solution)/shard_map/all_to_all | solution.py:113
  404.2 9.7 %all_gather.22 = bf16[128,1024]{1,0:T(8,128)(2,1)S(1)} all-gather(bf16[128,256]{1,0:T(8,128)(2,1)S(1)} %get-tuple-element.11), channel_id=1, replica_groups=mesh['sel'=64,'mdl'=4] {'mdl'}, dimensions={1}, use_global_device_ids=true | all-gather | bytes 327680 | tf_op jit(solution)/shard_map/all_gather | solution.py:82
  414.6 9.1 %all-gather = bf16[64,1024]{1,0:T(8,128)(2,1)S(1)} all-gather(bf16[64,256]{1,0:T(8,128)(2,1)S(1)} %gather_fusion.2), channel_id=2, replica_groups=mesh['sel'=64,'mdl'=4] {'mdl'}, dimensions={1}, use_global_device_ids=true | all-gather | bytes 163840 | tf_op jit(solution)/shard_map/all_gather | solution.py:115
  423.9 3.9 fusion.10
  429.3 7.8 %all-reduce.4 = (f32[128]{0:T(128)S(1)}, f32[128]{0:T(128)S(1)}, f32[64]{0:T(128)S(1)}, f32[64]{0:T(128)S(1)}) all-reduce(f32[128]{0:T(128)S(1)} %get-tuple-element.10, f32[128]{0:T(128)S(1)} %fusion.10, f32[64]{0:T(128)S(1)} %multiply_reduce_fusion.3, f32[64]{0:T(128)S(1)} %fusion.11), channel_id=1, replica_groups=mesh['sel'=64,'mdl'=4] {'mdl'}, use_global_device_ids=true, to_apply=%region_8.0 | all-reduce | flops 384 | bytes 3072 | tf_op jit(solution)/shard_map/psum | solution.py:83
  (95 shorter events, 38.0 us)
Async XLA Ops:
  7.2 156.1 %copy-start = (bf16[1408,256]{1,0:T(8,128)(2,1)S(1)}, bf16[1408,256]{1,0:T(8,128)(2,1)}, u32[]{:S(2)}) copy-start(bf16[1408,256]{1,0:T(8,128)(2,1)} %param.10) | copy-start | bytes 2162692
  7.2 74.2 %all-gather.7.cloned.1.call-start = ((), (), s32[]{:S(2)}) async-start(), calls=%async_computation.7 | async-start | bytes 2703360 | tf_op jit(solution)/shard_map/all_gather | solution.py:35
  50.6 113.6 %reduce-scatter.4.cloned.1.call-start = ((), (), s32[]{:S(2)}) async-start(), calls=%async_computation.8 | async-start | bytes 5406720 | tf_op jit(solution)/shard_map/reduce_scatter | solution.py:42
  87.8 2.2 copy-start.7
  99.1 11.8 %copy-start.4 = (bf16[384,352]{0,1:T(8,128)(2,1)S(1)}, bf16[384,352]{0,1:T(8,128)(2,1)}, u32[]{:S(2)}) copy-start(bf16[384,352]{0,1:T(8,128)(2,1)} %param.15) | copy-start | bytes 811012
  99.9 18.2 %all-to-all-start.4 = ((s32[64,2,1]{1,2,0:T(1,128)}), s32[64,2,1]{1,2,0:T(1,128)S(1)}, u32[]{:S(2)}, u32[]{:S(2)}) async-start(s32[64,2,1]{1,2,0:T(1,128)} %bitcast.2), calls=%async_computation.5 | async-start | bytes 65536 | tf_op jit(solution)/shard_map/all_to_all | solution.py:108
  111.4 40.8 %copy-start.5 = (bf16[128,256]{1,0:T(8,128)(2,1)S(1)}, bf16[128,256]{1,0:T(8,128)(2,1)}, u32[]{:S(2)}) copy-start(bf16[128,256]{1,0:T(8,128)(2,1)} %param.9) | copy-start | bytes 196612
  118.2 29.7 %all-to-all-start.3 = ((bf16[128,6,352]{2,1,0:T(8,128)(2,1)}), bf16[128,6,352]{2,1,0:T(8,128)(2,1)S(1)}, u32[]{:S(2)}, u32[]{:S(2)}) async-start(bf16[128,6,352]{2,1,0:T(8,128)(2,1)} %gather_fusion.5), calls=%async_computation.4 | async-start | bytes 1572864 | tf_op jit(solution)/shard_map/all_to_all | solution.py:107
  125.0 39.2 %copy-start.2 = (bf16[768,352]{0,1:T(8,128)(2,1)S(1)}, bf16[768,352]{0,1:T(8,128)(2,1)}, u32[]{:S(2)}) copy-start(bf16[768,352]{0,1:T(8,128)(2,1)} %copy.37) | copy-start | bytes 1622020
  125.0 72.7 %all-gather.9.cloned.1.call-start = ((), (), s32[]{:S(2)}) async-start(), calls=%async_computation.9 | async-start | bytes 2703360 | tf_op jit(solution)/shard_map/all_gather | solution.py:36
  151.5 272.3 %all-gather.5.cloned.1.call-start = ((), (), s32[]{:S(2)}) async-start(), calls=%async_computation.6 | async-start | bytes 4259840 | tf_op jit(solution)/shard_map/all_gather | solution.py:81
  211.2 171.8 %copy-start.6 = (u32[256]{0:T(256)S(1)}, u32[256]{0:T(256)}, u32[]{:S(2)}) copy-start(u32[256]{0:T(256)} %constant.52) | copy-start | bytes 3076
  346.4 34.1 %collective-permute-start.5 = (f32[6,1536]{1,0:T(8,128)S(1)}, f32[6,1536]{1,0:T(8,128)S(1)}, u32[]{:S(2)}, u32[]{:S(2)}) collective-permute-start(f32[6,1536]{1,0:T(8,128)S(1)} %slice.12), channel_id=1, source_target_pairs={{0,24},{4,28},{8,32},{12,36},{16,40},{20,44},{24,48},{28,52},{32,5... | collective-permute-start | bytes 110600
  350.3 34.0 %collective-permute-start.4 = (f32[24,1536]{1,0:T(8,128)S(1)}, f32[24,1536]{1,0:T(8,128)S(1)}, u32[]{:S(2)}, u32[]{:S(2)}) collective-permute-start(f32[24,1536]{1,0:T(8,128)S(1)} %fusion), channel_id=1, source_target_pairs={{0,20},{4,24},{8,28},{12,32},{16,36},{20,40},{24,44},{28,48},{32,5... | collective-permute-start | bytes 442376
  365.7 18.6 %collective-permute-start.3 = (f32[24,1536]{1,0:T(8,128)S(1)}, f32[24,1536]{1,0:T(8,128)S(1)}, u32[]{:S(2)}, u32[]{:S(2)}) collective-permute-start(f32[24,1536]{1,0:T(8,128)S(1)} %fusion), channel_id=1, source_target_pairs={{0,16},{4,20},{8,24},{12,28},{16,32},{20,36},{24,40},{28,44},{32,4... | collective-permute-start | bytes 442376
  367.7 16.7 %collective-permute-start.2 = (f32[24,1536]{1,0:T(8,128)S(1)}, f32[24,1536]{1,0:T(8,128)S(1)}, u32[]{:S(2)}, u32[]{:S(2)}) collective-permute-start(f32[24,1536]{1,0:T(8,128)S(1)} %fusion), channel_id=1, source_target_pairs={{0,12},{4,16},{8,20},{12,24},{16,28},{20,32},{24,36},{28,40},{32,4... | collective-permute-start | bytes 442376
  378.6 10.9 %collective-permute-start.1 = (f32[24,1536]{1,0:T(8,128)S(1)}, f32[24,1536]{1,0:T(8,128)S(1)}, u32[]{:S(2)}, u32[]{:S(2)}) collective-permute-start(f32[24,1536]{1,0:T(8,128)S(1)} %fusion), channel_id=1, source_target_pairs={{0,8},{4,12},{8,16},{12,20},{16,24},{20,28},{24,32},{28,36},{32,40... | collective-permute-start | bytes 442376
  380.6 9.0 %collective-permute-start = (f32[24,1536]{1,0:T(8,128)S(1)}, f32[24,1536]{1,0:T(8,128)S(1)}, u32[]{:S(2)}, u32[]{:S(2)}) collective-permute-start(f32[24,1536]{1,0:T(8,128)S(1)} %fusion), channel_id=1, source_target_pairs={{0,4},{4,8},{8,12},{12,16},{16,20},{20,24},{24,28},{28,32},{32,36}... | collective-permute-start | bytes 442376
  391.4 22.5 %all-to-all-start.2 = ((bf16[64,2,256]{2,1,0:T(2,128)(2,1)}), bf16[64,2,256]{2,1,0:T(2,128)(2,1)S(1)}, u32[]{:S(2)}, u32[]{:S(2)}) async-start(bf16[64,2,256]{2,1,0:T(2,128)(2,1)} %all_to_all.41), calls=%async_computation.3 | async-start | bytes 131072 | tf_op jit(solution)/shard_map/all_to_all | solution.py:113
  423.9 4.0 copy-start.3
  437.1 1.3 copy-start.1
Sparse Core Ops, SparseCore 0:
  50.7 30.5 all-gather.6
  99.3 50.5 reduce-scatter.3
  151.7 36.5 all-gather.8
  197.9 79.8 all-gather.4
where the time goes:
time: 453 us; the launch traced here: 445 us
  blocking collectives  234 us (52%)
  starting transfers between devices  66.1 us (15%)
  waiting for transfers between devices  62.3 us (14%)
  matrix products  35.8 us (8%)
  local copies, waits for them, and re-layouts  20.8 us (5%)
  between operations  15.5 us (3%)
  other arithmetic  10.2 us (2%)
    unnamed x1, blocking collectives  135 us
    unnamed x6, starting transfers between devices  36.5 us
    all_to_all x1, blocking collectives, per_device(): lax.all_to_all(pad_tok, 'sel', split_axis=0, concat_axis=0, tiled=True)  35 us
    all_gather x1, waiting for transfers between devices, learn(): lax.all_gather(kept_tok.reshape(n_rows, d_part), 'mdl', axis=1, tiled=True)  30.7 us
    all_to_all x1, waiting for transfers between devices, per_device(): lax.all_to_all(pad_cot, 'sel', split_axis=0, concat_axis=0, tiled=True)  21.1 us
    dot_general x1, matrix products, learn(): lax.dot_general(tok_full, grad_pre, (((0,), (0,)), ((), ())), preferred_e...  13.5 us
    all_gather x1, blocking collectives, learn(): pooled_full = lax.all_gather(pooled, 'mdl', axis=1, tiled=True)  12.2 us
    all_to_all x1, starting transfers between devices, per_device(): lax.all_to_all(slot_hat, 'sel', split_axis=0, concat_axis=0, tiled=True)  11.5 us
  transfers between devices with their start and end apart: 13, of which 4 were waited for; matrix products, arithmetic and copies ran while one was open for 38% of the time, Pallas kernels for 0%

commit v1 on v0

v1 whole, which is shorter than its diff:
```python
import jax
import jax.numpy as jnp
from jax import lax
from jax.sharding import PartitionSpec as P

logit_scale = 64.0
eps = 1e-06


def gelu_parts(pre_act):
    cumul = 0.5 * (1.0 + lax.erf(pre_act * 0.7071067811865476))
    density = jnp.exp(-0.5 * pre_act * pre_act) * 0.3989422804014327
    return (pre_act * cumul, cumul + pre_act * density)


def partial_scores(rows_hat, text_all):
    return lax.dot_general(
        rows_hat, text_all, (((1,), (1,)), ((), ())), preferred_element_type=jnp.float32
    )


def exp_total(rows_full, text_share):
    return jnp.sum(jnp.exp(logit_scale * partial_scores(rows_full, text_share)), axis=1)


def own_product(rows_part, texts_part):
    return jnp.sum(rows_part.astype(jnp.float32) * texts_part.astype(jnp.float32), axis=1)


def learn(kept_tok, kept_cot, row_weight, w_up, w_down, ref_proj):
    n_patch, n_items, d_part = kept_tok.shape
    n_rows = n_items * n_patch
    tok_full = lax.all_gather(kept_tok.reshape(n_rows, d_part), "mdl", axis=1, tiled=True)
    cot_full = lax.all_gather(kept_cot.reshape(n_rows, d_part), "mdl", axis=1, tiled=True)
    pre_act = jnp.dot(tok_full, w_up, preferred_element_type=jnp.float32)
    activated, gelu_slope = gelu_parts(pre_act)
    hidden = activated.astype(jnp.bfloat16).reshape(n_patch, n_items, -1)
    hidden_mean = jnp.mean(hidden, axis=0, dtype=jnp.float32).astype(jnp.bfloat16)
    mixed_part = jnp.dot(hidden_mean, w_down, preferred_element_type=jnp.float32)
    summed = lax.psum_scatter(mixed_part, "mdl", scatter_dimension=1, tiled=True)
    tok_mean = jnp.mean(kept_tok, axis=0, dtype=jnp.float32)
    pooled = (summed + tok_mean).astype(jnp.bfloat16)
    pooled_full = lax.all_gather(pooled, "mdl", axis=1, tiled=True)
    learn_emb = jnp.dot(pooled_full, ref_proj, preferred_element_type=jnp.float32)
    learn_sq = lax.psum(jnp.sum(learn_emb * learn_emb, axis=1), "mdl")
    learn_hat = (learn_emb * lax.rsqrt(learn_sq + eps)[:, None]).astype(jnp.bfloat16)
    grad_act = lax.dot_general(
        cot_full, w_down, (((1,), (1,)), ((), ())), preferred_element_type=jnp.float32
    )
    row_w = jnp.tile(row_weight, n_patch)[:, None]
    grad_pre = (grad_act * row_w * gelu_slope).astype(jnp.bfloat16)
    grad_part = lax.dot_general(
        tok_full, grad_pre, (((0,), (0,)), ((), ())), preferred_element_type=jnp.float32
    ).astype(jnp.bfloat16)
    grad_up = lax.psum_scatter(grad_part, "sel", scatter_dimension=0, tiled=True)
    return (learn_hat, grad_up.astype(jnp.float32))


def per_device(patches, text, ref_proj, w_up, w_down, kept_index, dest, cotan):
    n_sel = lax.axis_size("sel")
    ex_dev = text.shape[0]
    d_part = patches.shape[1]
    n_patch = patches.shape[0] // ex_dev
    k_dev = kept_index.shape[0]
    blocks = patches.reshape(ex_dev, n_patch, d_part)
    pooled = jnp.mean(blocks, axis=1, dtype=jnp.float32).astype(jnp.bfloat16)
    pooled_full = lax.all_gather(pooled, "mdl", axis=1, tiled=True)
    img_emb = jnp.dot(pooled_full, ref_proj, preferred_element_type=jnp.float32)
    text_vals = text.astype(jnp.float32)
    img_sq, text_sq = lax.psum(
        (jnp.sum(img_emb * img_emb, axis=1), jnp.sum(text_vals * text_vals, axis=1)), "mdl"
    )
    img_hat = (img_emb * lax.rsqrt(img_sq + eps)[:, None]).astype(jnp.bfloat16)
    text_hat = (text_vals * lax.rsqrt(text_sq + eps)[:, None]).astype(jnp.bfloat16)
    text_rows = lax.all_to_all(text_hat, "mdl", split_axis=0, concat_axis=1, tiled=True)
    text_split = lax.all_gather(text_rows, "sel", axis=0, tiled=True)
    img_full = lax.all_gather(img_hat, "mdl", axis=1, tiled=True)
    ref_total, ref_own = lax.psum(
        (exp_total(img_full, text_split), own_product(img_hat, text_hat)), "mdl"
    )
    ref_loss = jnp.log(ref_total) - logit_scale * ref_own
    kept_tok = blocks[kept_index].transpose(1, 0, 2)
    kept_cot = cotan.reshape(k_dev, n_patch, d_part).transpose(1, 0, 2)
    onehot = (dest[:, None] == jnp.arange(n_sel, dtype=jnp.int32)[None, :]).astype(jnp.float32)
    counts = lax.psum(jnp.sum(onehot, axis=0), "sel")
    row_weight = 1.0 / jnp.sum(onehot * counts[None, :], axis=1)
    kept_hat, grad_up = learn(kept_tok, kept_cot, row_weight, w_up, w_down, ref_proj)
    learn_full = lax.all_gather(kept_hat, "mdl", axis=1, tiled=True)
    learn_total, learn_own = lax.psum(
        (exp_total(learn_full, text_split), own_product(kept_hat, text_hat[kept_index])), "mdl"
    )
    learner_loss = jnp.log(learn_total) - logit_scale * learn_own
    learnability = learner_loss - ref_loss[kept_index]
    return (ref_loss, learnability, grad_up)


def solution(mesh):
    in_specs = (
        P("sel", "mdl"),
        P("sel", "mdl"),
        P(None, "mdl"),
        P(None, "mdl"),
        P("mdl", None),
        P("sel"),
        P("sel"),
        P("sel", "mdl"),
    )
    out_specs = (P("sel"), P("sel"), P("sel", "mdl"))
    return jax.shard_map(
        per_device, mesh=mesh, in_specs=in_specs, out_specs=out_specs, check_vma=False
    )
```

time: 453 us -> 461 us (1.018)
  blocking collectives: 234 us -> 298 us
  starting transfers between devices: 66.1 us -> 52.1 us
  waiting for transfers between devices: 62.3 us -> 48.5 us
  local copies, waits for them, and re-layouts: 20.8 us -> 9.77 us
  matrix products: 35.8 us -> 26 us
  other arithmetic: 10.2 us -> 3.73 us
    psum x0 -> x1, blocking collectives: none -> 112 us  [per_device(): counts = lax.psum(jnp.sum(onehot, axis=0), 'sel')]
    all_to_all x1 -> x0, blocking collectives: 35 us -> none  [per_device(): lax.all_to_all(pad_tok, 'sel', split_axis=0, concat_axis=0, tiled=True)]
    all_to_all x3 -> x0, starting transfers between devices: 29.4 us -> none  [the longest x1 11.5 us: per_device(): lax.all_to_all(slot_hat, 'sel', split_axis=0, concat_axis=0, tiled=True)]
    all_to_all x3 -> x0, waiting for transfers between devices: 26.3 us -> none  [the longest x1 21.1 us: per_device(): lax.all_to_all(pad_cot, 'sel', split_axis=0, concat_axis=0, tiled=True)]
    unnamed x6 -> x7, starting transfers between devices: 36.5 us -> 52 us
    unnamed x10 -> x11, waiting for transfers between devices: 5.3 us -> 20.1 us
    dot_general x1 -> x0, matrix products: 9.11 us -> none  [learn(): mixed_part = jnp.dot(hidden, w_down, preferred_element_type=jnp.float32)]
    unnamed x1, blocking collectives: 135 us -> 127 us
  transfers between devices with their start and end apart: 13 -> 10, of which waited for: 4 -> 3; matrix products, arithmetic and copies ran while one was open for 38% -> 32% of each run, Pallas kernels for 0% -> 0%
where the time goes in v1:
time: 461 us; the launch traced here: 453 us
  blocking collectives  298 us (65%)
  starting transfers between devices  52.1 us (11%)
  waiting for transfers between devices  48.5 us (11%)
  matrix products  26 us (6%)
  between operations  14.8 us (3%)
  local copies, waits for them, and re-layouts  9.77 us (2%)
    unnamed x1, blocking collectives  127 us
    psum x1, blocking collectives, per_device(): counts = lax.psum(jnp.sum(onehot, axis=0), 'sel')  112 us
    unnamed x7, starting transfers between devices  52 us
    all_gather x1, waiting for transfers between devices, learn(): lax.all_gather(kept_tok.reshape(n_rows, d_part), 'mdl', axis=1, tiled=True)  28.5 us
    unnamed x11, waiting for transfers between devices  20.1 us
    all_gather x1, blocking collectives, per_device(): pooled_full = lax.all_gather(pooled, 'mdl', axis=1, tiled=True)  10.8 us
    all_gather x1, blocking collectives, per_device(): img_full = lax.all_gather(img_hat, 'mdl', axis=1, tiled=True)  9.84 us
    all_gather x1, blocking collectives, learn(): pooled_full = lax.all_gather(pooled, 'mdl', axis=1, tiled=True)  9.24 us
  transfers between devices with their start and end apart: 10, of which 3 were waited for; matrix products, arithmetic and copies ran while one was open for 32% of the time, Pallas kernels for 0%

profile of v1, /device:TPU:25, one launch (start us, length us, event | category | flops | bytes accessed | tf_op | source)
XLA Modules:
  0.0 453.3 jit_solution(5215248771271861127)
XLA Ops:
  8.0 1.4 copy.43
  11.2 28.5 %all-gather.7.cloned.1.call-done = bf16[384,1408]{0,1:T(8,128)(2,1)} async-done(((bf16[384,352]{0,1:T(8,128)(2,1)}), bf16[384,1408]{0,1:T(8,128)(2,1)}) %all-gather.7.cloned.1.call-update) | async-done | bytes 1081360 | tf_op jit(solution)/shard_map/all_gather | solution.py:33
  39.7 6.3 %multiply_convert_fusion = (bf16[384,1536]{1,0:T(8,128)(2,1)S(1)}, f32[384,1536]{1,0:T(8,128)}) fusion(bf16[384,1408]{0,1:T(8,128)(2,1)} %all-gather.7.cloned.1.call-done, bf16[1408,1536]{1,0:T(8,128)(2,1)} %param.11), kind=kOutput, calls=%fused_computation.16 | convolution fusion | flops 1663893504 | bytes 8945664 | tf_op jit(solution)/shard_map/dot_general | solution.py:35
  46.1 5.0 %convolution_bitcast_fusion = f32[1408,64]{1,0:T(8,128)} fusion(bf16[1536,1408]{1,0:T(8,128)(2,1)} %param.12, f32[64,1536]{1,0:T(8,128)S(1)} %convert_reduce_fusion), kind=kOutput, calls=%fused_computation.8 | convolution fusion | flops 277020672 | bytes 5079040
  53.7 10.8 %all_gather.21 = bf16[128,1408]{0,1:T(8,128)(2,1)S(1)} all-gather(bf16[128,352]{0,1:T(8,128)(2,1)S(1)} %multiply_convert_fusion.3), channel_id=1, replica_groups=mesh['sel'=64,'mdl'=4] {'mdl'}, dimensions={1}, use_global_device_ids=true | all-gather | bytes 450560 | tf_op jit(solution)/shard_map/all_gather | solution.py:67
  64.9 11.6 %reduce-scatter.6.cloned.1.call-done = f32[352,64]{1,0:T(8,128)} async-done(((f32[1408,64]{1,0:T(8,128)}), f32[352,64]{1,0:T(8,128)}) %reduce-scatter.6.cloned.1.call-update) | async-done | bytes 90128
  77.5 9.2 %all-gather = bf16[4,352,64]{1,2,0:T(8,128)(2,1)S(1)} all-gather(bf16[1,352,64]{1,2,0:T(8,128)(2,1)S(1)} %fusion.14), channel_id=1, replica_groups=mesh['sel'=64,'mdl'=4] {'mdl'}, dimensions={0}, use_global_device_ids=true | all-gather | bytes 225280 | tf_op jit(solution)/shard_map/all_gather | solution.py:43
  87.5 6.5 %all-reduce.3 = (f32[128]{0:T(128)S(1)}, f32[128]{0:T(128)S(1)}, f32[64]{0:T(128)S(1)}) all-reduce(f32[128]{0:T(128)S(1)} %fusion.12, f32[128]{0:T(128)S(1)} %get-tuple-element.15, f32[64]{0:T(128)S(1)} %get-tuple-element.19), channel_id=1, replica_groups=mesh['sel'=64,'mdl'=4] {'mdl'}, use_global_device_ids=true, to_apply=%region_4.0 | all-reduce | flops 320 | bytes 2560 | tf_op jit(solution)/shard_map/psum | solution.py:70
  94.2 7.3 %all_to_all.19 = bf16[4,32,256]{2,1,0:T(8,128)(2,1)S(1)} all-to-all(bf16[4,32,256]{2,1,0:T(8,128)(2,1)S(1)} %bitcast.38), channel_id=1, replica_groups=mesh['sel'=64,'mdl'=4] {'mdl'}, dimensions={0} | all-to-all | bytes 131072 | tf_op jit(solution)/shard_map/all_to_all | solution.py:75
  102.2 111.7 %psum.63 = f32[64]{0:T(128)S(1)} all-reduce(f32[64]{0:T(128)S(1)} %convert_reduce_fusion.3), channel_id=1, replica_groups=mesh['sel'=64,'mdl'=4] {'sel'}, use_global_device_ids=true, to_apply=%region_19.0 | all-reduce | flops 64 | bytes 512 | tf_op jit(solution)/shard_map/psum | solution.py:85
  214.2 8.6 %convolution_convert_fusion = bf16[1408,1536]{1,0:T(8,128)(2,1)} fusion(bf16[384,1408]{0,1:T(8,128)(2,1)S(1)} %copy-done.6, bf16[384,1408]{0,1:T(8,128)(2,1)} %all-gather.9.cloned.1.call-done, bf16[1536,1408]{1,0:T(8,128)(2,1)} %param.12, f32[384,1536]{1,0:T(8,128)} %get-tuple-element.18, f32[384]{0:T(512)S(1)} %mul.143), kind=kOutput, calls=%fused_computation.3 | convolution fusion | flops 3330539520 | bytes 13174272 | tf_op jit(solution)/shard_map/dot_general | solution.py:52
  222.7 127.3 %fusion = bf16[24,1536]{1,0:T(8,128)(2,1)S(1)} fusion(bf16[1408,1536]{1,0:T(8,128)(2,1)} %convolution_convert_fusion), kind=kCustom, calls=%all-reduce-scatter | all-reduce-scatter fusion | flops 2359297 | bytes 4400128
  350.1 18.8 %collective-permute-start.5 = (bf16[6,1536]{1,0:T(8,128)(2,1)S(1)}, bf16[6,1536]{1,0:T(8,128)(2,1)S(1)}, u32[]{:S(2)}, u32[]{:S(2)}) collective-permute-start(bf16[6,1536]{1,0:T(8,128)(2,1)S(1)} %slice.6), channel_id=1, source_target_pairs={{0,24},{4,28},{8,32},{12,36},{16,40},{20,44},{24,48},{28,52},{32,5... | collective-permute-start | bytes 55304
  368.9 7.0 %collective-permute-start = (bf16[24,1536]{1,0:T(8,128)(2,1)S(1)}, bf16[24,1536]{1,0:T(8,128)(2,1)S(1)}, u32[]{:S(2)}, u32[]{:S(2)}) collective-permute-start(bf16[24,1536]{1,0:T(8,128)(2,1)S(1)} %fusion), channel_id=1, source_target_pairs={{0,4},{4,8},{8,12},{12,16},{16,20},{20,24},{24,28},{28,32},{32,36}... | collective-permute-start | bytes 221192
  375.9 7.5 %collective-permute-start.1 = (bf16[24,1536]{1,0:T(8,128)(2,1)S(1)}, bf16[24,1536]{1,0:T(8,128)(2,1)S(1)}, u32[]{:S(2)}, u32[]{:S(2)}) collective-permute-start(bf16[24,1536]{1,0:T(8,128)(2,1)S(1)} %fusion), channel_id=1, source_target_pairs={{0,8},{4,12},{8,16},{12,20},{16,24},{20,28},{24,32},{28,36},{32,40... | collective-permute-start | bytes 221192
  383.4 9.3 %collective-permute-start.2 = (bf16[24,1536]{1,0:T(8,128)(2,1)S(1)}, bf16[24,1536]{1,0:T(8,128)(2,1)S(1)}, u32[]{:S(2)}, u32[]{:S(2)}) collective-permute-start(bf16[24,1536]{1,0:T(8,128)(2,1)S(1)} %fusion), channel_id=1, source_target_pairs={{0,12},{4,16},{8,20},{12,24},{16,28},{20,32},{24,36},{28,40},{32,4... | collective-permute-start | bytes 221192
  392.6 7.2 %collective-permute-start.3 = (bf16[24,1536]{1,0:T(8,128)(2,1)S(1)}, bf16[24,1536]{1,0:T(8,128)(2,1)S(1)}, u32[]{:S(2)}, u32[]{:S(2)}) collective-permute-start(bf16[24,1536]{1,0:T(8,128)(2,1)S(1)} %fusion), channel_id=1, source_target_pairs={{0,16},{4,20},{8,24},{12,28},{16,32},{20,36},{24,40},{28,44},{32,4... | collective-permute-start | bytes 221192
  399.9 2.2 collective-permute-start.4
  403.4 8.4 %collective-permute-done.4 = bf16[24,1536]{1,0:T(8,128)(2,1)S(1)} collective-permute-done((bf16[24,1536]{1,0:T(8,128)(2,1)S(1)}, bf16[24,1536]{1,0:T(8,128)(2,1)S(1)}, u32[]{:S(2)}, u32[]{:S(2)}) %collective-permute-start.4) | collective-permute-done | bytes 73760
  414.4 9.1 %all_gather.26 = bf16[64,1024]{1,0:T(8,128)(2,1)S(1)} all-gather(bf16[64,256]{1,0:T(8,128)(2,1)S(1)} %get-tuple-element.11), channel_id=1, replica_groups=mesh['sel'=64,'mdl'=4] {'mdl'}, dimensions={1}, use_global_device_ids=true | all-gather | bytes 163840 | tf_op jit(solution)/shard_map/all_gather | solution.py:88
  423.5 9.8 %all_gather.22 = bf16[128,1024]{1,0:T(8,128)(2,1)S(1)} all-gather(bf16[128,256]{1,0:T(8,128)(2,1)S(1)} %get-tuple-element.13), channel_id=1, replica_groups=mesh['sel'=64,'mdl'=4] {'mdl'}, dimensions={1}, use_global_device_ids=true | all-gather | bytes 327680 | tf_op jit(solution)/shard_map/all_gather | solution.py:77
  433.3 3.9 fusion.10
  437.2 1.6 fusion.9
  438.8 6.6 %all-reduce.2 = (f32[128]{0:T(128)S(1)}, f32[128]{0:T(128)S(1)}, f32[64]{0:T(128)S(1)}, f32[64]{0:T(128)S(1)}) all-reduce(f32[128]{0:T(128)S(1)} %get-tuple-element.12, f32[128]{0:T(128)S(1)} %fusion.9, f32[64]{0:T(128)S(1)} %get-tuple-element.10, f32[64]{0:T(128)S(1)} %fusion.10), channel_id=1, replica_groups=mesh['sel'=64,'mdl'=4] {'mdl'}, use_global_device_ids=true, to_apply=%region_8.0 | all-reduce | flops 384 | bytes 3072 | tf_op jit(solution)/shard_map/psum | solution.py:78
  (71 shorter events, 13.1 us)
Async XLA Ops:
  7.2 57.3 %copy-start = (bf16[1408,256]{1,0:T(8,128)(2,1)S(1)}, bf16[1408,256]{1,0:T(8,128)(2,1)}, u32[]{:S(2)}) copy-start(bf16[1408,256]{1,0:T(8,128)(2,1)} %param.10) | copy-start | bytes 2162692
  7.2 32.5 %all-gather.7.cloned.1.call-start = ((), (), s32[]{:S(2)}) async-start(), calls=%async_computation.3 | async-start | bytes 1351680 | tf_op jit(solution)/shard_map/all_gather | solution.py:33
  11.2 65.3 %reduce-scatter.6.cloned.1.call-start = ((), (), s32[]{:S(2)}) async-start(), calls=%async_computation.5 | async-start | bytes 901120
  46.1 5.1 %copy-start.3 = (bf16[384,352]{0,1:T(8,128)(2,1)S(1)}, bf16[384,352]{0,1:T(8,128)(2,1)}, u32[]{:S(2)}) copy-start(bf16[384,352]{0,1:T(8,128)(2,1)} %param.15) | copy-start | bytes 811012
  51.1 2.1 copy-start.4
  51.2 163.0 %all-gather.9.cloned.1.call-start = ((), (), s32[]{:S(2)}) async-start(), calls=%async_computation.4 | async-start | bytes 1351680 | tf_op jit(solution)/shard_map/all_gather | solution.py:34
  52.5 380.8 %all-gather.5.cloned.1.call-start = ((), (), s32[]{:S(2)}) async-start(), calls=%async_computation.2 | async-start | bytes 4259840 | tf_op jit(solution)/shard_map/all_gather | solution.py:76
  53.7 48.5 %copy-start.7 = (s32[64]{0:T(128)S(1)}, s32[64]{0:T(128)}, u32[]{:S(2)}) copy-start(s32[64]{0:T(128)} %param.14) | copy-start | bytes 772
  53.7 160.5 %copy-start.6 = (bf16[384,1408]{0,1:T(8,128)(2,1)S(1)}, bf16[384,1408]{0,1:T(8,128)(2,1)}, u32[]{:S(2)}) copy-start(bf16[384,1408]{0,1:T(8,128)(2,1)} %all-gather.7.cloned.1.call-done) | copy-start | bytes 3244036
  222.7 179.3 %copy-start.5 = (u32[256]{0:T(256)S(1)}, u32[256]{0:T(256)}, u32[]{:S(2)}) copy-start(u32[256]{0:T(256)} %constant.10) | copy-start | bytes 3076
  350.1 49.8 %collective-permute-start.5 = (bf16[6,1536]{1,0:T(8,128)(2,1)S(1)}, bf16[6,1536]{1,0:T(8,128)(2,1)S(1)}, u32[]{:S(2)}, u32[]{:S(2)}) collective-permute-start(bf16[6,1536]{1,0:T(8,128)(2,1)S(1)} %slice.6), channel_id=1, source_target_pairs={{0,24},{4,28},{8,32},{12,36},{16,40},{20,44},{24,48},{28,52},{32,5... | collective-permute-start | bytes 55304
  368.9 34.4 %collective-permute-start = (bf16[24,1536]{1,0:T(8,128)(2,1)S(1)}, bf16[24,1536]{1,0:T(8,128)(2,1)S(1)}, u32[]{:S(2)}, u32[]{:S(2)}) collective-permute-start(bf16[24,1536]{1,0:T(8,128)(2,1)S(1)} %fusion), channel_id=1, source_target_pairs={{0,4},{4,8},{8,12},{12,16},{16,20},{20,24},{24,28},{28,32},{32,36}... | collective-permute-start | bytes 221192
  375.9 27.5 %collective-permute-start.1 = (bf16[24,1536]{1,0:T(8,128)(2,1)S(1)}, bf16[24,1536]{1,0:T(8,128)(2,1)S(1)}, u32[]{:S(2)}, u32[]{:S(2)}) collective-permute-start(bf16[24,1536]{1,0:T(8,128)(2,1)S(1)} %fusion), channel_id=1, source_target_pairs={{0,8},{4,12},{8,16},{12,20},{16,24},{20,28},{24,32},{28,36},{32,40... | collective-permute-start | bytes 221192
  383.4 20.0 %collective-permute-start.2 = (bf16[24,1536]{1,0:T(8,128)(2,1)S(1)}, bf16[24,1536]{1,0:T(8,128)(2,1)S(1)}, u32[]{:S(2)}, u32[]{:S(2)}) collective-permute-start(bf16[24,1536]{1,0:T(8,128)(2,1)S(1)} %fusion), channel_id=1, source_target_pairs={{0,12},{4,16},{8,20},{12,24},{16,28},{20,32},{24,36},{28,40},{32,4... | collective-permute-start | bytes 221192
  392.6 10.7 %collective-permute-start.3 = (bf16[24,1536]{1,0:T(8,128)(2,1)S(1)}, bf16[24,1536]{1,0:T(8,128)(2,1)S(1)}, u32[]{:S(2)}, u32[]{:S(2)}) collective-permute-start(bf16[24,1536]{1,0:T(8,128)(2,1)S(1)} %fusion), channel_id=1, source_target_pairs={{0,16},{4,20},{8,24},{12,28},{16,32},{20,36},{24,40},{28,44},{32,4... | collective-permute-start | bytes 221192
  399.9 11.9 %collective-permute-start.4 = (bf16[24,1536]{1,0:T(8,128)(2,1)S(1)}, bf16[24,1536]{1,0:T(8,128)(2,1)S(1)}, u32[]{:S(2)}, u32[]{:S(2)}) collective-permute-start(bf16[24,1536]{1,0:T(8,128)(2,1)S(1)} %fusion), channel_id=1, source_target_pairs={{0,20},{4,24},{8,28},{12,32},{16,36},{20,40},{24,44},{28,48},{32,5... | collective-permute-start | bytes 221192
  433.3 3.9 copy-start.2
  445.4 1.3 copy-start.1
Sparse Core Ops, SparseCore 0:
  11.3 28.3 all-gather.6
  51.3 25.1 reduce-scatter.5
  78.3 26.5 all-gather.8
  107.5 79.5 all-gather.4

commit v2 on v1

v2 whole, which is shorter than its diff:
```python
import jax
import jax.numpy as jnp
from jax import lax
from jax.experimental import pallas as pl
from jax.experimental.pallas import tpu as pltpu
from jax.sharding import PartitionSpec as P

logit_scale = 64.0
eps = 1e-06
MESH = pl.DeviceIdType.MESH
f32 = jnp.float32
bf16 = jnp.bfloat16

NX, NY, NZ, NC = 4, 4, 8, 2
D, DP = 1408, 352
FH = 768
EMB, EP = 1024, 256
PATCH, E, K = 6, 128, 64
R = K * PATCH
G = 384
CH = 48
CA = 384
TB = E // NX

POS = {0: 0, 1: 1, 7: 2, 2: 3, 6: 4, 3: 5, 5: 6, 4: 7}
GROUPS = [(0, 1), (1, 2), (3, 2), (5, 2), (7, 1)]

N_COPIES = 112
N_LOCAL = 3


def dot(a, b):
    return lax.dot_general(a, b, (((1,), (0,)), ((), ())), preferred_element_type=f32)


def dot_nt(a, b):
    return lax.dot_general(a, b, (((1,), (1,)), ((), ())), preferred_element_type=f32)


def iota(shape, axis):
    return lax.broadcasted_iota(jnp.int32, shape, axis)


def one_hot(mask):
    return jnp.where(mask, 1.0, 0.0).astype(bf16)


def pool_mask(n_out, n_in):
    first = PATCH * iota((n_out, n_in), 0)
    col = iota((n_out, n_in), 1)
    return (col >= first) & (col < first + PATCH)


def spread(row):
    first = PATCH * iota((R, K), 1)
    line = iota((R, K), 0)
    return jnp.sum(jnp.where((line >= first) & (line < first + PATCH), row, 0.0), axis=1, keepdims=True)


def to_row(col, lanes):
    n = col.shape[0]
    return jnp.sum(jnp.where(iota((n, lanes), 0) == iota((n, lanes), 1), col, 0.0), axis=0, keepdims=True)


def to_col(row, n):
    lanes = row.shape[1]
    return jnp.sum(jnp.where(iota((n, lanes), 0) == iota((n, lanes), 1), row, 0.0), axis=1, keepdims=True)


SCRATCH = dict(
    proj=((D, EP), bf16),
    wup=((D, FH), bf16),
    wdn=((FH, D), bf16),
    wdt=((D, FH), bf16),
    tok=((2, NX, R, DP), bf16),
    cot=((2, NX, R, DP), bf16),
    pre=((2, R, FH), f32),
    act=((2, R, FH), f32),
    hid=((2 * R, FH), bf16),
    tokt=((NX, G, 2 * R), bf16),
    gpre=((2 * R, FH), bf16),
    tx=((NX, TB, EP), bf16),
    txt=((2 * NY, NZ * TB, EMB), bf16),
    dst=((2, 8, 128), f32),
    hz=((NZ, 8, 128), f32),
    hy=((NY, 8, 128), f32),
    mb=((2, NX, K, DP), f32),
    mr=((NX, K, DP), f32),
    mx=((NX, K, DP), f32),
    mxr=((NX, K, DP), f32),
    lpb=((NX, K, DP), bf16),
    leb=((NX, K, EP), bf16),
    lhat=((K, EMB), bf16),
    pb=((NX, E, DP), bf16),
    eb=((NX, E, EP), bf16),
    ihat=((E, EMB), bf16),
    rs=((NX, 8, 128), f32),
    ls=((NX, 8, 128), f32),
    ga=((NY, G, CA), f32),
    gb=((NY, G, FH - CA), f32),
    a1=((G, CA), f32),
    b1=((NY, CH, FH - CA), f32),
    sbp=((4, NY, CH, FH - CA), bf16),
    sbm=((4, NY, CH, FH - CA), bf16),
    rbp=((4, NY, CH, FH - CA), bf16),
    rbm=((4, NY, CH, FH - CA), bf16),
    sap=((2, G, CA), bf16),
    sam=((2, G, CA), bf16),
    rap=((2, G, CA), bf16),
    ram=((2, G, CA), bf16),
    szp=((4, CH, CA), bf16),
    szm=((3, CH, CA), bf16),
    rzp=((4, CH, CA), bf16),
    rzm=((3, CH, CA), bf16),
    syp=((2, CH, FH - CA), bf16),
    sym=((1, CH, FH - CA), bf16),
    ryp=((2, CH, FH - CA), bf16),
    rym=((1, CH, FH - CA), bf16),
    res=((CH, FH), f32),
    fin=((CH // 2, FH), f32),
)


def kernel(patches, text, cotan, kidx, dest, proj_hbm, wup_hbm, wdn_hbm, ref_out, learn_out, grad_out, *scratch):
    names = list(SCRATCH)
    s = dict(zip(names, scratch[: len(names)]))
    send_sem, recv_sem, local_sem = scratch[len(names) :]

    x = lax.axis_index("mdl")
    sel = lax.axis_index("sel")
    c = lax.rem(sel, NC)
    z = lax.rem(lax.div(sel, NC), NZ)
    y = lax.div(sel, NC * NZ)

    def dev(dx=0, dy=0, dz=0, dc=0):
        yy = lax.rem(y + dy, NY)
        zz = lax.rem(z + dz, NZ)
        cc = lax.rem(c + dc, NC)
        return {"sel": (yy * NZ + zz) * NC + cc, "mdl": lax.rem(x + dx, NX)}

    sib = dev(dc=1)
    xr = [None] + [dev(dx=r) for r in range(1, NX)]
    yp, ym, zp, zm = dev(dy=1), dev(dy=NY - 1), dev(dz=1), dev(dz=NZ - 1)
    partners = [sib, xr[1], xr[2], xr[3], yp, ym, zp, zm]

    copies = []

    def send(src, dst, device):
        i = len(copies)
        copy = pltpu.make_async_remote_copy(
            src_ref=src,
            dst_ref=dst,
            send_sem=send_sem.at[i],
            recv_sem=recv_sem.at[i],
            device_id=device,
            device_id_type=MESH,
        )
        copy.start()
        copies.append(copy)
        return copy

    def xblock(slot):
        return pl.ds(pl.multiple_of(lax.rem(x + NX - slot, NX) * DP, 32), DP)

    barrier = pltpu.get_barrier_semaphore()
    for p in partners:
        pl.semaphore_signal(barrier, inc=1, device_id=p, device_id_type=MESH)
    half = pl.multiple_of(c * FH, FH)
    loads = [
        pltpu.make_async_copy(wdn_hbm.at[pl.ds(half, FH), :], s["wdn"], local_sem.at[0]),
        pltpu.make_async_copy(wup_hbm.at[:, pl.ds(half, FH)], s["wup"], local_sem.at[1]),
        pltpu.make_async_copy(proj_hbm, s["proj"], local_sem.at[2]),
    ]
    for load in loads:
        load.start()

    kf = kidx[...].astype(f32)
    krow = spread(kf)
    line = iota((R, 1), 0).astype(f32)
    entry = spread(iota((1, K), 1).astype(f32))
    want = (PATCH * krow + (line - PATCH * entry)).astype(jnp.int32)
    s["tok"][0, 0] = dot(one_hot(iota((R, E * PATCH), 1) == want), patches[...]).astype(bf16)
    s["cot"][0, 0] = cotan[...]
    s["dst"][0] = jnp.zeros((8, 128), f32)
    s["dst"][0, 0:1, 0:K] = dest[...].astype(f32)

    pl.semaphore_wait(barrier, len(partners))

    text_cp = [
        send(text.at[pl.ds(pl.multiple_of(lax.rem(x + r, NX) * TB, TB), TB), :], s["tx"].at[r], xr[r])
        for r in range(1, NX)
    ]
    dst_cp = send(s["dst"].at[0], s["dst"].at[1], sib)

    def ring_start(buf):
        return (
            send(buf.at[0, 0], buf.at[0, 1], xr[1]),
            send(buf.at[0, 0], buf.at[0, 3], xr[3]),
            send(buf.at[0, 0], buf.at[1, 0], sib),
        )

    def ring_forward(buf, first):
        first[0].wait_recv()
        first[1].wait_recv()
        return (
            send(buf.at[0, 1, pl.ds(0, R // 2), :], buf.at[0, 2, pl.ds(0, R // 2), :], xr[1]),
            send(buf.at[0, 3, pl.ds(R // 2, R // 2), :], buf.at[0, 2, pl.ds(R // 2, R // 2), :], xr[3]),
        )

    tok1 = ring_start(s["tok"])

    loads[0].wait()
    eye = one_hot(iota((128, 128), 0) == iota((128, 128), 1))
    for j in range(D // 128):
        s["wdt"][j * 128 : (j + 1) * 128, :] = dot_nt(eye, s["wdn"][:, j * 128 : (j + 1) * 128]).astype(bf16)
    loads[1].wait()

    s["tx"][0] = text[pl.ds(pl.multiple_of(x * TB, TB), TB), :]
    for cp in text_cp:
        cp.wait_recv()
    tv = [s["tx"][r].astype(f32) for r in range(NX)]
    tsq = sum(jnp.sum(v * v, axis=1, keepdims=True) for v in tv)
    tinv = lax.rsqrt(tsq + eps)
    for r in range(NX):
        s["txt"][0, 0:TB, r * EP : (r + 1) * EP] = (tv[r] * tinv).astype(bf16)

    dst_cp.wait_recv()
    lane = iota((K, 128), 1).astype(f32)
    chip_hist = jnp.zeros((1, 128), f32)
    for sh in range(2):
        dcol = to_col(s["dst"][sh, 0:1, :], K)
        chip_hist += jnp.sum(jnp.where(lane == dcol, 1.0, 0.0), axis=0, keepdims=True)
    s["hz"][0] = jnp.broadcast_to(chip_hist, (8, 128))

    def tz(slot):
        return s["txt"].at[0, pl.ds(POS[slot] * TB, TB), :]

    def z_step(t):
        out = [
            (send(tz(t - 1), tz(t), zp), send(s["hz"].at[t - 1], s["hz"].at[t], zp)),
        ]
        if t < NZ // 2:
            a, b = (NZ - t + 1) % NZ, NZ - t
            out.append((send(tz(a), tz(b), zm), send(s["hz"].at[a], s["hz"].at[b], zm)))
        return out

    def z_wait(step):
        for cp, hcp in step:
            cp.wait_recv()
            hcp.wait_recv()

    def yg(slot, g):
        first, n = GROUPS[g]
        return s["txt"].at[slot, pl.ds(first * TB, n * TB), :]

    def y_first(g):
        return (send(yg(0, g), yg(1, g), yp), send(yg(0, g), yg(3, g), ym))

    zs1 = z_step(1)
    ys = [y_first(0)]

    def up(sh, slot):
        part = dot(s["tok"][sh, slot], s["wup"][xblock(slot), :])
        s["pre"][sh] = part if slot == 0 else s["pre"][sh] + part

    up(0, 0)
    z_wait(zs1)
    zs2 = z_step(2)
    ys.append(y_first(1))
    tok1[2].wait_recv()
    up(1, 0)
    s["pb"][0] = (dot(one_hot(pool_mask(E, E * PATCH)), patches[...]) * (1.0 / PATCH)).astype(bf16)
    z_wait(zs2)
    zs3 = z_step(3)
    ys.append(y_first(2))

    tok2 = ring_forward(s["tok"], tok1)
    cot1 = ring_start(s["cot"])
    tokc = [send(s["tok"].at[0, i], s["tok"].at[1, i], sib) for i in (1, 3)]
    up(0, 1)
    z_wait(zs3)
    zs4 = z_step(4)
    ys.append(y_first(3))
    up(0, 3)
    tokc[0].wait_recv()
    up(1, 1)
    tokc[1].wait_recv()
    up(1, 3)
    z_wait(zs4)
    ys.append(y_first(4))
    txt_c = [send(s["txt"].at[0], s["txt"].at[NY], sib)]
    s["hy"][0] = sum(s["hz"][i] for i in range(NZ))
    hy1 = (send(s["hy"].at[0], s["hy"].at[1], yp), send(s["hy"].at[0], s["hy"].at[3], ym))

    tok2[0].wait_recv()
    tok2[1].wait_recv()
    tokc2 = send(s["tok"].at[0, 2], s["tok"].at[1, 2], sib)
    up(0, 2)
    tokc2.wait_recv()
    up(1, 2)

    for sh in range(2):

        def act_step(i, carry):
            rows = pl.ds(pl.multiple_of(i * 32, 32), 32)
            v = s["pre"][sh, rows, :]
            cumul = 0.5 * (1.0 + lax.erf(v * 0.7071067811865476))
            density = jnp.exp(-0.5 * v * v) * 0.3989422804014327
            s["hid"][pl.ds(pl.multiple_of(sh * R + i * 32, 32), 32), :] = (v * cumul).astype(bf16)
            s["pre"][sh, rows, :] = cumul + v * density
            return carry

        lax.fori_loop(0, R // 32, act_step, 0)

    gi, gj = iota((G, DP), 0), iota((G, DP), 1)
    base = 22 * lax.div(gi, 24)
    inner = lax.rem(gi, 24)
    place = one_hot((inner < 22) & (gj == base + inner))
    for slot in range(NX):
        for sh in range(2):
            s["tokt"][slot, :, sh * R : (sh + 1) * R] = dot_nt(place, s["tok"][sh, slot]).astype(bf16)

    hy1[0].wait_recv()
    hy1[1].wait_recv()
    hy2 = send(s["hy"].at[1], s["hy"].at[2], yp)
    for g in range(5):
        ys[g][0].wait_recv()
        ys[g][1].wait_recv()
    ys2 = [send(yg(1, g), yg(2, g), yp) for g in (0, 1, 4)]
    ys2 += [send(yg(3, g), yg(2, g), ym) for g in (2, 3)]
    txt_c += [send(s["txt"].at[i], s["txt"].at[NY + i], sib) for i in (1, 3)]

    pooled_h = dot(one_hot(pool_mask(2 * K, 2 * R)), s["hid"][...]) * (1.0 / PATCH)
    pooled_h = pooled_h.astype(bf16)
    for slot in range(NX):
        m = dot_nt(pooled_h, s["wdt"][xblock(slot), :])
        s["mb"][0, slot] = m[0:K]
        s["mb"][1, slot] = m[K : 2 * K]
    m_c = send(s["mb"].at[1], s["mr"], sib)

    def back(sh, slot):
        part = dot(s["cot"][sh, slot], s["wdt"][xblock(slot), :])
        s["act"][sh] = part if slot == 0 else s["act"][sh] + part

    back(0, 0)
    cot1[2].wait_recv()
    back(1, 0)
    cot2 = ring_forward(s["cot"], cot1)
    cotc = [send(s["cot"].at[0, i], s["cot"].at[1, i], sib) for i in (1, 3)]
    pb_cp = [send(s["pb"].at[0], s["pb"].at[r], xr[r]) for r in range(1, NX)]
    back(0, 1)
    back(0, 3)
    cotc[0].wait_recv()
    back(1, 1)
    cotc[1].wait_recv()
    back(1, 3)

    hy2.wait_recv()
    counts = sum(s["hy"][i][0:1, :] for i in range(NY))
    lane_r = iota((R, 128), 1).astype(f32)
    weight = []
    for sh in range(2):
        drow = spread(s["dst"][sh, 0:1, 0:K])
        weight.append(1.0 / jnp.sum(jnp.where(lane_r == drow, counts, 0.0), axis=1, keepdims=True))

    m_c.wait_recv()
    for slot in range(NX):
        s["mx"][slot] = s["mb"][0, slot] + s["mr"][slot]
    mx_cp = [send(s["mx"].at[NX - r], s["mxr"].at[r], xr[r]) for r in range(1, NX)]

    cot2[0].wait_recv()
    cot2[1].wait_recv()
    cotc2 = send(s["cot"].at[0, 2], s["cot"].at[1, 2], sib)
    back(0, 2)
    cotc2.wait_recv()
    back(1, 2)
    for sh in range(2):
        s["gpre"][sh * R : (sh + 1) * R, :] = (s["act"][sh] * weight[sh] * s["pre"][sh]).astype(bf16)

    def slot_of(delta):
        return lax.rem(x + 2 * NY - y - delta, NX)

    def zrows(zeta):
        return pl.ds(pl.multiple_of(lax.rem(z + zeta, NZ) * CH, 16), CH)

    for delta in range(NY):
        s["gb"][delta] = dot(s["tokt"][slot_of(delta)], s["gpre"][:, CA:FH])

    def b_step(t, before):
        sp, sm, rp, rm = s["sbp"], s["sbm"], s["rbp"], s["rbm"]
        if t == 1:
            for delta in (0, 1):
                sp[0, delta] = s["gb"][delta, zrows(4), :].astype(bf16)
            for delta in (2, 3):
                sm[0, delta] = s["gb"][delta, zrows(4), :].astype(bf16)
            return (
                send(sp.at[0, pl.ds(0, 2)], rp.at[0, pl.ds(0, 2)], zp),
                send(sm.at[0, pl.ds(2, 2)], rm.at[0, pl.ds(2, 2)], zm),
            )
        before[0].wait_recv()
        before[1].wait_recv()
        for delta in range(NY):
            vp = s["gb"][delta, zrows(5 - t), :]
            vm = s["gb"][delta, zrows(3 + t), :]
            if t > 2 or delta < 2:
                vp = vp + rp[t - 2, delta].astype(f32)
            if t > 2 or delta >= 2:
                vm = vm + rm[t - 2, delta].astype(f32)
            sp[t - 1, delta] = vp.astype(bf16)
            sm[t - 1, delta] = vm.astype(bf16)
        return send(sp.at[t - 1], rp.at[t - 1], zp), send(sm.at[t - 1], rm.at[t - 1], zm)

    bs = b_step(1, None)

    def ga(delta):
        s["ga"][delta] = dot(s["tokt"][slot_of(delta)], s["gpre"][:, 0:CA])

    ga(2)
    hg = G // 2
    s["sap"][0, 0:hg, :] = s["ga"][2, 0:hg, :].astype(bf16)
    s["sam"][0, hg:G, :] = s["ga"][2, hg:G, :].astype(bf16)
    as1 = (
        send(s["sap"].at[0, pl.ds(0, hg)], s["rap"].at[0, pl.ds(0, hg)], yp),
        send(s["sam"].at[0, pl.ds(hg, hg)], s["ram"].at[0, pl.ds(hg, hg)], ym),
    )
    ga(1)
    ga(3)
    ga(0)

    for cp in ys2:
        cp.wait_recv()
    txt_c.append(send(s["txt"].at[2], s["txt"].at[NY + 2], sib))

    bs = b_step(2, bs)

    for cp in mx_cp:
        cp.wait_recv()
    tok_mean = dot(one_hot(pool_mask(K, R)), s["tok"][0, 0]) * (1.0 / PATCH)
    mixed = s["mx"][0] + s["mxr"][1] + s["mxr"][2] + s["mxr"][3]
    s["lpb"][0] = (tok_mean + mixed).astype(bf16)
    lp_cp = [send(s["lpb"].at[0], s["lpb"].at[r], xr[r]) for r in range(1, NX)]

    as1[0].wait_recv()
    as1[1].wait_recv()
    s["sap"][1, 0:hg, :] = (s["ga"][1, 0:hg, :] + s["rap"][0, 0:hg, :].astype(f32)).astype(bf16)
    s["sap"][1, hg:G, :] = s["ga"][1, hg:G, :].astype(bf16)
    s["sam"][1, 0:hg, :] = s["ga"][3, 0:hg, :].astype(bf16)
    s["sam"][1, hg:G, :] = (s["ga"][3, hg:G, :] + s["ram"][0, hg:G, :].astype(f32)).astype(bf16)
    as2 = (send(s["sap"].at[1], s["rap"].at[1], yp), send(s["sam"].at[1], s["ram"].at[1], ym))

    loads[2].wait()
    for cp in pb_cp:
        cp.wait_recv()
    emb = sum(dot(s["pb"][slot], s["proj"][xblock(slot), :]) for slot in range(NX))
    s["eb"][0] = emb.astype(bf16)
    eb_cp = [send(s["eb"].at[0], s["eb"].at[r], xr[r]) for r in range(1, NX)]

    bs = b_step(3, bs)

    for cp in lp_cp:
        cp.wait_recv()
    emb = sum(dot(s["lpb"][slot], s["proj"][xblock(slot), :]) for slot in range(NX))
    s["leb"][0] = emb.astype(bf16)
    le_cp = [send(s["leb"].at[0], s["leb"].at[r], xr[r]) for r in range(1, NX)]

    def normalise(blocks, out):
        v = [blocks[slot].astype(f32) for slot in range(NX)]
        inv = lax.rsqrt(sum(jnp.sum(e * e, axis=1, keepdims=True) for e in v) + eps)
        for slot in range(NX):
            out[:, slot * EP : (slot + 1) * EP] = (v[slot] * inv).astype(bf16)

    def exp_total(hat):
        n = hat.shape[0]

        def step(i, acc):
            return acc + jnp.exp(logit_scale * dot_nt(hat[...], s["txt"][i]))

        acc = lax.fori_loop(0, 2 * NY, step, jnp.zeros((n, NZ * TB), f32))
        return jnp.sum(acc, axis=1, keepdims=True)

    def own_product(hat, own_col):
        scores = dot_nt(hat[...], s["txt"][0, 0:TB, :])
        mine = own_col == (iota(scores.shape, 1) + x * TB)
        return jnp.sum(jnp.where(mine, scores, 0.0), axis=1, keepdims=True)

    def share(buf, total, own):
        buf[0] = jnp.zeros((8, 128), f32)
        buf[0, 0:1, :] = to_row(total, 128)
        buf[0, 1:2, :] = to_row(own, 128)
        return [send(buf.at[0], buf.at[r], xr[r]) for r in range(1, NX)]

    def loss_row(buf, cps):
        for cp in cps:
            cp.wait_recv()
        tile = buf[0] + buf[1] + buf[2] + buf[3]
        return jnp.log(tile[0:1, :]) - logit_scale * tile[1:2, :]

    for cp in eb_cp:
        cp.wait_recv()
    normalise(s["eb"], s["ihat"])
    for cp in txt_c:
        cp.wait_recv()
    r_cp = share(s["rs"], exp_total(s["ihat"]), own_product(s["ihat"], iota((E, 1), 0)))

    bs = b_step(4, bs)

    as2[0].wait_recv()
    as2[1].wait_recv()
    s["a1"][...] = s["ga"][0] + s["rap"][1].astype(f32) + s["ram"][1].astype(f32)

    def a_step(t, before):
        vp = s["a1"][zrows(5 - t), :]
        if t > 1:
            before[0].wait_recv()
            vp = vp + s["rzp"][t - 2].astype(f32)
        s["szp"][t - 1] = vp.astype(bf16)
        out = [send(s["szp"].at[t - 1], s["rzp"].at[t - 1], zp)]
        if t < 4:
            vm = s["a1"][zrows(4 + t), :]
            if t > 1:
                before[1].wait_recv()
                vm = vm + s["rzm"][t - 2].astype(f32)
            s["szm"][t - 1] = vm.astype(bf16)
            out.append(send(s["szm"].at[t - 1], s["rzm"].at[t - 1], zm))
        return out

    az1 = a_step(1, None)

    for cp in le_cp:
        cp.wait_recv()
    normalise(s["leb"], s["lhat"])
    kcol = to_col(kf, K)
    l_cp = share(s["ls"], exp_total(s["lhat"]), own_product(s["lhat"], kcol.astype(jnp.int32)))

    az2 = a_step(2, az1)

    bs[0].wait_recv()
    bs[1].wait_recv()
    for delta in range(NY):
        s["b1"][delta] = s["gb"][delta, zrows(0), :] + s["rbp"][3, delta].astype(f32) + s["rbm"][3, delta].astype(f32)
    s["syp"][0] = s["b1"][2].astype(bf16)
    s["sym"][0] = s["b1"][3].astype(bf16)
    by1 = (send(s["syp"].at[0], s["ryp"].at[0], yp), send(s["sym"].at[0], s["rym"].at[0], ym))

    az3 = a_step(3, az2)

    by1[0].wait_recv()
    s["syp"][1] = (s["b1"][1] + s["ryp"][0].astype(f32)).astype(bf16)
    by2 = send(s["syp"].at[1], s["ryp"].at[1], yp)

    az4 = a_step(4, az3)

    ref_row = loss_row(s["rs"], r_cp)
    ref_out[...] = ref_row
    learn_row = loss_row(s["ls"], l_cp)
    picked = jnp.sum(jnp.where(iota((K, E), 1).astype(f32) == kcol, ref_row, 0.0), axis=1, keepdims=True)
    learn_out[...] = learn_row[:, 0:K] - to_row(picked, K)

    by1[1].wait_recv()
    by2.wait_recv()
    s["res"][:, CA:FH] = s["b1"][0] + s["ryp"][1].astype(f32) + s["rym"][0].astype(f32)
    az3[1].wait_recv()
    az4[0].wait_recv()
    s["res"][:, 0:CA] = s["a1"][zrows(0), :] + s["rzp"][3].astype(f32) + s["rzm"][2].astype(f32)

    other = pl.ds(pl.multiple_of((1 - c) * (CH // 2), 8), CH // 2)
    fin = send(s["res"].at[other, :], s["fin"], sib)
    mine = s["res"][pl.ds(pl.multiple_of(c * (CH // 2), 8), CH // 2), :][0:22, :]
    fin.wait_recv()
    theirs = s["fin"][0:22, :]
    grad_out[:, 0:FH] = jnp.where(c == 0, mine, theirs)
    grad_out[:, FH : 2 * FH] = jnp.where(c == 0, theirs, mine)

    for cp in copies:
        cp.wait_send()


def per_device(patches, text, ref_proj, w_up, w_down, kept_index, dest, cotan):
    vmem = pl.BlockSpec(memory_space=pltpu.VMEM)
    hbm = pl.BlockSpec(memory_space=pl.ANY)
    scratch = [pltpu.VMEM(shape, dtype) for shape, dtype in SCRATCH.values()]
    scratch += [
        pltpu.SemaphoreType.DMA((N_COPIES,)),
        pltpu.SemaphoreType.DMA((N_COPIES,)),
        pltpu.SemaphoreType.DMA((N_LOCAL,)),
    ]
    ref_loss, learnability, grad_up = pl.pallas_call(
        kernel,
        out_shape=(
            jax.ShapeDtypeStruct((1, E), f32),
            jax.ShapeDtypeStruct((1, K), f32),
            jax.ShapeDtypeStruct((22, 2 * FH), f32),
        ),
        in_specs=[vmem] * 5 + [hbm] * 3,
        out_specs=(vmem, vmem, vmem),
        scratch_shapes=scratch,
        compiler_params=pltpu.CompilerParams(
            collective_id=0, has_side_effects=True, vmem_limit_bytes=56 * 1024 * 1024
        ),
        name="contrastive_step",
    )(patches, text, cotan, kept_index.reshape(1, K), dest.reshape(1, K), ref_proj, w_up, w_down)
    return (ref_loss.reshape(E), learnability.reshape(K), grad_up)


def solution(mesh):
    in_specs = (
        P("sel", "mdl"),
        P("sel", "mdl"),
        P(None, "mdl"),
        P(None, "mdl"),
        P("mdl", None),
        P("sel"),
        P("sel"),
        P("sel", "mdl"),
    )
    out_specs = (P("sel"), P("sel"), P("sel", "mdl"))
    return jax.shard_map(
        per_device, mesh=mesh, in_specs=in_specs, out_specs=out_specs, check_vma=False
    )
```

time: 461 us -> 91.2 us (0.20); the launches traced: 453 us -> 89.4 us
  blocking collectives: 298 us -> 0 us
  Pallas kernels: 0 us -> 80.9 us
  starting transfers between devices: 52.1 us -> 0 us
  waiting for transfers between devices: 48.5 us -> 0 us
  matrix products: 26 us -> 0 us
  between operations: 14.8 us -> 0.64 us
    unnamed x1 -> x0, blocking collectives: 127 us -> none
    psum x3 -> x0, blocking collectives: 125 us -> none  [the longest x1 112 us: per_device(): counts = lax.psum(jnp.sum(onehot, axis=0), 'sel')]
    pallas_call x0 -> x1, Pallas kernels: none -> 80.9 us  [per_device(): pl.pallas_call(kernel, out_shape=(jax.ShapeDtypeStruct((1, E), f32), jax....]
    unnamed x7 -> x0, starting transfers between devices: 52 us -> none
    all_gather x4 -> x0, blocking collectives: 39 us -> none  [the longest x1 10.8 us: per_device(): pooled_full = lax.all_gather(pooled, 'mdl', axis=1, tiled=True)]
    all_gather x3 -> x0, waiting for transfers between devices: 28.5 us -> none  [the longest x1 28.5 us: learn(): lax.all_gather(kept_tok.reshape(n_rows, d_part), 'mdl', axis=1, tiled=True)]
    dot_general x6 -> x0, matrix products: 21.1 us -> none  [the longest x1 8.58 us: learn(): lax.dot_general(tok_full, grad_pre, (((0,), (0,)), ((), ())), preferred_e...]
    unnamed x11 -> x0, waiting for transfers between devices: 20.1 us -> none
  transfers between devices with their start and end apart: 10 -> 0, of which waited for: 3 -> 0; matrix products, arithmetic and copies ran while one was open for 32% -> 0% of each run, Pallas kernels for 0% -> 0%
where the time goes in v2:
time: 91.2 us; the launch traced here: 89.4 us
  Pallas kernels  80.9 us (89%)
  local copies, waits for them, and re-layouts  7.83 us (9%)
    pallas_call x1, Pallas kernels, per_device(): pl.pallas_call(kernel, out_shape=(jax.ShapeDtypeStruct((1, E), f32), jax....  80.9 us
    unnamed x5, local copies, waits for them, and re-layouts  7.83 us

profile of v2, /device:TPU:25, one launch (start us, length us, event | category | flops | bytes accessed | tf_op | source)
XLA Modules:
  0.0 89.4 jit_solution(2316290226785508181)
XLA Ops:
  0.6 1.9 %copy.12.cotan = bf16[384,352]{1,0:T(8,128)(2,1)} copy(bf16[384,352]{0,1:T(8,128)(2,1)} %param.15) | data formatting | bytes 540672 | tf_op args[7]
  2.5 2.1 %copy.11.patches = bf16[768,352]{1,0:T(8,128)(2,1)} copy(bf16[768,352]{0,1:T(8,128)(2,1)} %param.8) | data formatting | bytes 1081344 | tf_op args[0]
  4.6 80.9 %contrastive_step.1 = (f32[1,128]{1,0:T(1,128)}, f32[1,64]{1,0:T(1,128)}, f32[22,1536]{1,0:T(8,128)}) custom-call(bf16[768,352]{1,0:T(8,128)(2,1)} %copy.11.patches, bf16[128,256]{1,0:T(8,128)(2,1)} %text.1, bf16[384,352]{1,0:T(8,128)(2,1)} %copy.12.cotan, s32[1,64]{1,0:T(1,128)} %bitcast.4, s32[1,64]{1,0:T(1,128)} %bitcast.5, bf16[1408,256]{1,0:T(8,128)(2,1)} %proj_hbm.1, ...), custom_call_target="tpu_custom_call" | custom-call | tf_op jit(solution)/shard_map/contrastive_step/pallas_call | solution.py:587
  85.5 1.2 %copy.16 = f32[128]{0:T(128)} copy(f32[128]{0:T(128)} %bitcast.7) | data formatting | bytes 1024
  86.7 1.1 %copy.17 = f32[64]{0:T(128)} copy(f32[64]{0:T(128)} %bitcast.6) | data formatting | bytes 512
  87.8 1.6 %copy.18 = f32[22,1536]{1,0:T(8,128)} copy(f32[22,1536]{1,0:T(8,128)} %get-tuple-element.14) | data formatting | bytes 270336

commit v3 on v2

v3 whole, which is shorter than its diff:
```python
import jax
import jax.numpy as jnp
from jax import lax
from jax.experimental import pallas as pl
from jax.experimental.pallas import tpu as pltpu
from jax.sharding import PartitionSpec as P

logit_scale = 64.0
eps = 1e-06
MESH = pl.DeviceIdType.MESH
f32 = jnp.float32
bf16 = jnp.bfloat16

NX, NY, NZ, NC = 4, 4, 8, 2
D, DP = 1408, 352
FH = 768
EMB, EP = 1024, 256
PATCH, E, K = 6, 128, 64
R = K * PATCH
G = 384
CH = 48
CA = 384
TB = E // NX

POS = {0: 0, 1: 1, 7: 2, 2: 3, 6: 4, 3: 5, 5: 6, 4: 7}
GROUPS = [(0, 1), (1, 2), (3, 2), (5, 2), (7, 1)]

N_COPIES = 150
N_LOCAL = 3


def dot(a, b):
    return lax.dot_general(a, b, (((1,), (0,)), ((), ())), preferred_element_type=f32)


def dot_tn(a, b):
    return lax.dot_general(a, b, (((0,), (0,)), ((), ())), preferred_element_type=f32)


def dot_nt(a, b):
    return lax.dot_general(a, b, (((1,), (1,)), ((), ())), preferred_element_type=f32)


def iota(shape, axis):
    return lax.broadcasted_iota(jnp.int32, shape, axis)


def one_hot(mask):
    return jnp.where(mask, 1.0, 0.0).astype(bf16)


def pool_mask(n_out, n_in):
    first = PATCH * iota((n_out, n_in), 0)
    col = iota((n_out, n_in), 1)
    return (col >= first) & (col < first + PATCH)


def spread(row):
    first = PATCH * iota((R, K), 1)
    line = iota((R, K), 0)
    return jnp.sum(jnp.where((line >= first) & (line < first + PATCH), row, 0.0), axis=1, keepdims=True)


def to_row(col, lanes):
    n = col.shape[0]
    return jnp.sum(jnp.where(iota((n, lanes), 0) == iota((n, lanes), 1), col, 0.0), axis=0, keepdims=True)


def to_col(row, n):
    lanes = row.shape[1]
    return jnp.sum(jnp.where(iota((n, lanes), 0) == iota((n, lanes), 1), row, 0.0), axis=1, keepdims=True)


SCRATCH = dict(
    proj=((D, EP), bf16),
    wup=((D, FH), bf16),
    wdn=((FH, D), bf16),
    wdt=((D, FH), bf16),
    tok=((2, NX, DP, R), bf16),
    cot=((2, NX, DP, R), bf16),
    pre=((2, R, FH), f32),
    act=((2, R, FH), f32),
    hid=((2 * R, FH), bf16),
    tokt=((NX, G, 2 * R), bf16),
    gpre=((2 * R, FH), bf16),
    tx=((NX, TB, EP), bf16),
    txt=((2 * NY, NZ * TB, EMB), bf16),
    dst=((2, 8, 128), f32),
    hz=((NZ, 8, 128), f32),
    hy=((NY, 8, 128), f32),
    mb=((2, NX, K, DP), f32),
    mr=((NX, K, DP), f32),
    mx=((NX, K, DP), f32),
    mxr=((NX, K, DP), f32),
    lpb=((NX, K, DP), bf16),
    leb=((NX, K, EP), bf16),
    lhat=((K, EMB), bf16),
    pb=((NX, E, DP), bf16),
    eb=((NX, E, EP), bf16),
    ihat=((E, EMB), bf16),
    rs=((NX, 8, 128), f32),
    ls=((NX, 8, 128), f32),
    ga=((NY, G, CA), f32),
    gb=((NY, G, FH - CA), f32),
    a1=((G, CA), f32),
    b1=((NY, CH, FH - CA), f32),
    sbp=((4, NY, CH, FH - CA), bf16),
    sbm=((4, NY, CH, FH - CA), bf16),
    rbp=((4, NY, CH, FH - CA), bf16),
    rbm=((4, NY, CH, FH - CA), bf16),
    sap=((2, G, CA), bf16),
    sam=((2, G, CA), bf16),
    rap=((2, G, CA), bf16),
    ram=((2, G, CA), bf16),
    sz=((NZ, CH, CA), bf16),
    rz=((NZ, CH, CA), bf16),
    sy=((NY, CH, FH - CA), bf16),
    ry=((NY, CH, FH - CA), bf16),
    res=((CH, FH), f32),
    fin=((CH // 2, FH), f32),
)


def kernel(patches, text, cotan, kidx, dest, proj_hbm, wup_hbm, wdn_hbm, loss_out, grad_out, *scratch):
    names = list(SCRATCH)
    s = dict(zip(names, scratch[: len(names)]))
    send_sem, recv_sem, local_sem = scratch[len(names) :]

    x = lax.axis_index("mdl")
    sel = lax.axis_index("sel")
    c = lax.rem(sel, NC)
    z = lax.rem(lax.div(sel, NC), NZ)
    y = lax.div(sel, NC * NZ)

    def dev(dx=0, dy=0, dz=0, dc=0):
        yy = lax.rem(y + dy, NY)
        zz = lax.rem(z + dz, NZ)
        cc = lax.rem(c + dc, NC)
        return {"sel": (yy * NZ + zz) * NC + cc, "mdl": lax.rem(x + dx, NX)}

    sib = dev(dc=1)
    xr = [None] + [dev(dx=r) for r in range(1, NX)]
    yr = [None] + [dev(dy=r) for r in range(1, NY)]
    zr = [None] + [dev(dz=r) for r in range(1, NZ)]
    yp, ym, zp, zm = yr[1], yr[NY - 1], zr[1], zr[NZ - 1]
    partners = [sib] + xr[1:] + yr[1:] + zr[1:]

    copies = []

    def send(src, dst, device):
        i = len(copies)
        copy = pltpu.make_async_remote_copy(
            src_ref=src,
            dst_ref=dst,
            send_sem=send_sem.at[i],
            recv_sem=recv_sem.at[i],
            device_id=device,
            device_id_type=MESH,
        )
        copy.start()
        copies.append(copy)
        return copy

    def xblock(slot):
        return pl.ds(pl.multiple_of(lax.rem(x + NX - slot, NX) * DP, 32), DP)

    barrier = pltpu.get_barrier_semaphore()
    for p in partners:
        pl.semaphore_signal(barrier, inc=1, device_id=p, device_id_type=MESH)
    half = pl.multiple_of(c * FH, FH)
    loads = [
        pltpu.make_async_copy(wdn_hbm.at[pl.ds(half, FH), :], s["wdn"], local_sem.at[0]),
        pltpu.make_async_copy(wup_hbm.at[:, pl.ds(half, FH)], s["wup"], local_sem.at[1]),
        pltpu.make_async_copy(proj_hbm, s["proj"], local_sem.at[2]),
    ]
    for load in loads:
        load.start()

    kf = kidx[...].astype(f32)
    krow = spread(kf)
    line = iota((R, 1), 0).astype(f32)
    entry = spread(iota((1, K), 1).astype(f32))
    want = (PATCH * krow + (line - PATCH * entry)).astype(jnp.int32)
    s["tok"][0, 0] = dot_nt(patches[...], one_hot(iota((R, E * PATCH), 1) == want)).astype(bf16)
    s["cot"][0, 0] = cotan[...]
    s["dst"][0] = jnp.zeros((8, 128), f32)
    s["dst"][0, 0:1, 0:K] = dest[...].astype(f32)

    pl.semaphore_wait(barrier, len(partners))

    text_cp = [
        send(text.at[pl.ds(pl.multiple_of(lax.rem(x + r, NX) * TB, TB), TB), :], s["tx"].at[r], xr[r])
        for r in range(1, NX)
    ]
    dst_cp = send(s["dst"].at[0], s["dst"].at[1], sib)

    h = DP // 2

    def half_to(buf, src, dst, part, device):
        rows = pl.ds(part * h, h)
        return send(buf.at[0, src, rows, :], buf.at[0, dst, rows, :], device)

    def ring_start(buf):
        first = (half_to(buf, 0, 1, 0, xr[1]), half_to(buf, 0, 3, 1, xr[3]))
        second = (half_to(buf, 0, 1, 1, xr[1]), half_to(buf, 0, 3, 0, xr[3]))
        return first, second

    def ring_forward(buf, first):
        out = []
        first[0].wait_recv()
        out.append(half_to(buf, 1, 2, 0, xr[1]))
        first[1].wait_recv()
        out.append(half_to(buf, 3, 2, 1, xr[3]))
        return out

    def wait_both(pair):
        pair[0].wait_recv()
        pair[1].wait_recv()

    def to_core(buf, slot):
        return send(buf.at[0, slot], buf.at[1, slot], sib)

    tok1 = ring_start(s["tok"])
    tokc0 = to_core(s["tok"], 0)
    cotc0 = to_core(s["cot"], 0)

    dst_cp.wait_recv()
    lane = iota((K, 128), 1).astype(f32)
    chip_hist = jnp.zeros((1, 128), f32)
    for sh in range(2):
        dcol = to_col(s["dst"][sh, 0:1, :], K)
        chip_hist += jnp.sum(jnp.where(lane == dcol, 1.0, 0.0), axis=0, keepdims=True)
    s["hz"][0] = jnp.broadcast_to(chip_hist, (8, 128))
    hz_cp = [send(s["hz"].at[0], s["hz"].at[r], zr[r]) for r in range(1, NZ)]

    loads[0].wait()
    eye = one_hot(iota((128, 128), 0) == iota((128, 128), 1))
    for j in range(D // 128):
        s["wdt"][j * 128 : (j + 1) * 128, :] = dot_nt(eye, s["wdn"][:, j * 128 : (j + 1) * 128]).astype(bf16)
    loads[1].wait()

    s["tx"][0] = text[pl.ds(pl.multiple_of(x * TB, TB), TB), :]
    for cp in text_cp:
        cp.wait_recv()
    tv = [s["tx"][r].astype(f32) for r in range(NX)]
    tsq = sum(jnp.sum(v * v, axis=1, keepdims=True) for v in tv)
    tinv = lax.rsqrt(tsq + eps)
    for r in range(NX):
        s["txt"][0, 0:TB, r * EP : (r + 1) * EP] = (tv[r] * tinv).astype(bf16)

    def tz(slot):
        return s["txt"].at[0, pl.ds(POS[slot] * TB, TB), :]

    def z_step(t):
        out = [send(tz(t - 1), tz(t), zp)]
        if t < NZ // 2:
            out.append(send(tz((NZ - t + 1) % NZ), tz(NZ - t), zm))
        return out

    def z_wait(step):
        for cp in step:
            cp.wait_recv()

    def yg(slot, g):
        first, n = GROUPS[g]
        return s["txt"].at[slot, pl.ds(first * TB, n * TB), :]

    def y_first(g):
        return (send(yg(0, g), yg(1, g), yp), send(yg(0, g), yg(3, g), ym))

    def up(sh, slot):
        part = dot_tn(s["tok"][sh, slot], s["wup"][xblock(slot), :])
        s["pre"][sh] = part if slot == 0 else s["pre"][sh] + part

    def back(sh, slot):
        part = dot_tn(s["cot"][sh, slot], s["wdt"][xblock(slot), :])
        s["act"][sh] = part if slot == 0 else s["act"][sh] + part

    zs1 = z_step(1)
    ys = [y_first(0)]
    up(0, 0)

    tok2 = ring_forward(s["tok"], tok1[0])
    cot1 = ring_start(s["cot"])
    for cp in hz_cp:
        cp.wait_recv()
    s["hy"][0] = sum(s["hz"][i] for i in range(NZ))
    hy_cp = [send(s["hy"].at[0], s["hy"].at[r], yr[r]) for r in range(1, NY)]
    tokc0.wait_recv()
    up(1, 0)
    z_wait(zs1)
    zs2 = z_step(2)
    ys.append(y_first(1))

    wait_both(tok1[1])
    tokc = [to_core(s["tok"], i) for i in (1, 3)]
    up(0, 1)
    up(0, 3)
    s["pb"][0] = (dot_nt(one_hot(pool_mask(E, E * PATCH)), patches[...]) * (1.0 / PATCH)).astype(bf16)
    wait_both(tokc)
    up(1, 1)
    up(1, 3)

    wait_both(tok2)
    tokc2 = to_core(s["tok"], 2)
    up(0, 2)
    z_wait(zs2)
    zs3 = z_step(3)
    ys.append(y_first(2))
    tokc2.wait_recv()
    up(1, 2)

    for sh in range(2):

        def act_step(i, carry):
            rows = pl.ds(pl.multiple_of(i * 32, 32), 32)
            v = s["pre"][sh, rows, :]
            cumul = 0.5 * (1.0 + lax.erf(v * 0.7071067811865476))
            density = jnp.exp(-0.5 * v * v) * 0.3989422804014327
            s["hid"][pl.ds(pl.multiple_of(sh * R + i * 32, 32), 32), :] = (v * cumul).astype(bf16)
            s["pre"][sh, rows, :] = cumul + v * density
            return carry

        lax.fori_loop(0, R // 32, act_step, 0)

    cot2 = ring_forward(s["cot"], cot1[0])
    pb_cp = [send(s["pb"].at[0], s["pb"].at[r], xr[r]) for r in range(1, NX)]

    pooled_h = dot(one_hot(pool_mask(2 * K, 2 * R)), s["hid"][...]) * (1.0 / PATCH)
    pooled_h = pooled_h.astype(bf16)
    for slot in range(NX):
        m = dot_nt(pooled_h, s["wdt"][xblock(slot), :])
        s["mb"][0, slot] = m[0:K]
        s["mb"][1, slot] = m[K : 2 * K]
    m_c = send(s["mb"].at[1], s["mr"], sib)

    back(0, 0)
    cotc0.wait_recv()
    back(1, 0)
    z_wait(zs3)
    zs4 = z_step(4)
    ys.append(y_first(3))

    for cp in hy_cp:
        cp.wait_recv()
    counts = sum(s["hy"][i][0:1, :] for i in range(NY))
    lane_r = iota((R, 128), 1).astype(f32)
    weight = []
    for sh in range(2):
        drow = spread(s["dst"][sh, 0:1, 0:K])
        weight.append(1.0 / jnp.sum(jnp.where(lane_r == drow, counts, 0.0), axis=1, keepdims=True))

    wait_both(cot1[1])
    cotc = [to_core(s["cot"], i) for i in (1, 3)]
    back(0, 1)
    back(0, 3)

    gi, gj = iota((G, DP), 0), iota((G, DP), 1)
    base = 22 * lax.div(gi, 24)
    inner = lax.rem(gi, 24)
    place = one_hot((inner < 22) & (gj == base + inner))
    for slot in range(NX):
        for sh in range(2):
            s["tokt"][slot, :, sh * R : (sh + 1) * R] = dot(place, s["tok"][sh, slot]).astype(bf16)

    m_c.wait_recv()
    for slot in range(NX):
        s["mx"][slot] = s["mb"][0, slot] + s["mr"][slot]
    mx_cp = [send(s["mx"].at[NX - r], s["mxr"].at[r], xr[r]) for r in range(1, NX)]

    wait_both(cotc)
    back(1, 1)
    back(1, 3)

    ys2 = []
    for g in (0, 1):
        wait_both(ys[g])
        ys2.append(send(yg(1, g), yg(2, g), yp))
    wait_both(ys[2])
    ys2.append(send(yg(3, 2), yg(2, 2), ym))

    wait_both(cot2)
    cotc2 = to_core(s["cot"], 2)
    back(0, 2)
    z_wait(zs4)
    ys.append(y_first(4))
    cotc2.wait_recv()
    back(1, 2)
    for sh in range(2):
        s["gpre"][sh * R : (sh + 1) * R, :] = (s["act"][sh] * weight[sh] * s["pre"][sh]).astype(bf16)

    def slot_of(delta):
        return lax.rem(x + 2 * NY - y - delta, NX)

    def zrows(zeta):
        return pl.ds(pl.multiple_of(lax.rem(z + zeta, NZ) * CH, 16), CH)

    for delta in range(NY):
        s["gb"][delta] = dot(s["tokt"][slot_of(delta)], s["gpre"][:, CA:FH])

    b_cp = {}

    def b_send(k, delta, up_z):
        out, got = (s["sbp"], s["rbp"]) if up_z else (s["sbm"], s["rbm"])
        value = s["gb"][delta, zrows(4 - k if up_z else 4 + k), :]
        first = 0 if (delta < 2) == up_z else 1
        if k > first:
            b_cp[up_z, k - 1, delta].wait_recv()
            value = value + got[k - 1, delta].astype(f32)
        out[k, delta] = value.astype(bf16)
        b_cp[up_z, k, delta] = send(out.at[k, delta], got.at[k, delta], zp if up_z else zm)

    def b_step(t):
        for i in (0, 1):
            b_send(t - 1, i, True)
            b_send(t - 1, 2 + i, False)
        if t < 4:
            for i in (0, 1):
                b_send(t, 2 + i, True)
                b_send(t, i, False)

    b_step(1)

    def ga(delta):
        s["ga"][delta] = dot(s["tokt"][slot_of(delta)], s["gpre"][:, 0:CA])

    ga(2)
    hg = G // 2
    s["sap"][0, 0:hg, :] = s["ga"][2, 0:hg, :].astype(bf16)
    s["sam"][0, hg:G, :] = s["ga"][2, hg:G, :].astype(bf16)
    as1 = (
        send(s["sap"].at[0, pl.ds(0, hg)], s["rap"].at[0, pl.ds(0, hg)], yp),
        send(s["sam"].at[0, pl.ds(hg, hg)], s["ram"].at[0, pl.ds(hg, hg)], ym),
    )
    ga(1)
    s["sap"][1, hg:G, :] = s["ga"][1, hg:G, :].astype(bf16)
    as2 = [send(s["sap"].at[1, pl.ds(hg, hg)], s["rap"].at[1, pl.ds(hg, hg)], yp)]
    ga(3)
    s["sam"][1, 0:hg, :] = s["ga"][3, 0:hg, :].astype(bf16)
    as2.append(send(s["sam"].at[1, pl.ds(0, hg)], s["ram"].at[1, pl.ds(0, hg)], ym))
    ga(0)

    txt_c = [send(s["txt"].at[0], s["txt"].at[NY], sib)]
    wait_both(ys[3])
    ys2.append(send(yg(3, 3), yg(2, 3), ym))
    wait_both(ys[4])
    ys2.append(send(yg(1, 4), yg(2, 4), yp))
    txt_c += [send(s["txt"].at[i], s["txt"].at[NY + i], sib) for i in (1, 3)]

    for cp in mx_cp:
        cp.wait_recv()
    tok_mean = dot_nt(one_hot(pool_mask(K, R)), s["tok"][0, 0]) * (1.0 / PATCH)
    mixed = s["mx"][0] + s["mxr"][1] + s["mxr"][2] + s["mxr"][3]
    s["lpb"][0] = (tok_mean + mixed).astype(bf16)
    lp_cp = [send(s["lpb"].at[0], s["lpb"].at[r], xr[r]) for r in range(1, NX)]

    b_step(2)

    loads[2].wait()
    for cp in pb_cp:
        cp.wait_recv()
    emb = sum(dot(s["pb"][slot], s["proj"][xblock(slot), :]) for slot in range(NX))
    s["eb"][0] = emb.astype(bf16)
    eb_cp = [send(s["eb"].at[0], s["eb"].at[r], xr[r]) for r in range(1, NX)]

    wait_both(as1)
    s["sap"][1, 0:hg, :] = (s["ga"][1, 0:hg, :] + s["rap"][0, 0:hg, :].astype(f32)).astype(bf16)
    as2.append(send(s["sap"].at[1, pl.ds(0, hg)], s["rap"].at[1, pl.ds(0, hg)], yp))
    s["sam"][1, hg:G, :] = (s["ga"][3, hg:G, :] + s["ram"][0, hg:G, :].astype(f32)).astype(bf16)
    as2.append(send(s["sam"].at[1, pl.ds(hg, hg)], s["ram"].at[1, pl.ds(hg, hg)], ym))

    b_step(3)

    for cp in lp_cp:
        cp.wait_recv()
    emb = sum(dot(s["lpb"][slot], s["proj"][xblock(slot), :]) for slot in range(NX))
    s["leb"][0] = emb.astype(bf16)
    le_cp = [send(s["leb"].at[0], s["leb"].at[r], xr[r]) for r in range(1, NX)]

    def normalise(blocks, out):
        v = [blocks[slot].astype(f32) for slot in range(NX)]
        inv = lax.rsqrt(sum(jnp.sum(e * e, axis=1, keepdims=True) for e in v) + eps)
        for slot in range(NX):
            out[:, slot * EP : (slot + 1) * EP] = (v[slot] * inv).astype(bf16)

    def exp_total(hat):
        n = hat.shape[0]

        def step(i, acc):
            return acc + jnp.exp(logit_scale * dot_nt(hat[...], s["txt"][i]))

        acc = lax.fori_loop(0, 2 * NY, step, jnp.zeros((n, NZ * TB), f32))
        return jnp.sum(acc, axis=1, keepdims=True)

    def own_product(hat, own_col):
        scores = dot_nt(hat[...], s["txt"][0, 0:TB, :])
        mine = own_col == (iota(scores.shape, 1) + x * TB)
        return jnp.sum(jnp.where(mine, scores, 0.0), axis=1, keepdims=True)

    def share(buf, total, own):
        buf[0] = jnp.zeros((8, 128), f32)
        buf[0, 0:1, :] = to_row(total, 128)
        buf[0, 1:2, :] = to_row(own, 128)
        return [send(buf.at[0], buf.at[r], xr[r]) for r in range(1, NX)]

    def loss_row(buf, cps):
        for cp in cps:
            cp.wait_recv()
        tile = buf[0] + buf[1] + buf[2] + buf[3]
        return jnp.log(tile[0:1, :]) - logit_scale * tile[1:2, :]

    for cp in eb_cp:
        cp.wait_recv()
    normalise(s["eb"], s["ihat"])
    for cp in ys2:
        cp.wait_recv()
    txt_c.append(send(s["txt"].at[2], s["txt"].at[NY + 2], sib))
    for cp in txt_c:
        cp.wait_recv()
    r_cp = share(s["rs"], exp_total(s["ihat"]), own_product(s["ihat"], iota((E, 1), 0)))

    b_step(4)

    for cp in as2:
        cp.wait_recv()
    s["a1"][...] = s["ga"][0] + s["rap"][1].astype(f32) + s["ram"][1].astype(f32)
    az = []
    for r in (4, 3, 5, 2, 6, 1, 7):
        s["sz"][r] = s["a1"][zrows(r), :].astype(bf16)
        az.append(send(s["sz"].at[r], s["rz"].at[r], zr[r]))

    for delta in range(NY):
        b_cp[True, 3, delta].wait_recv()
        b_cp[False, 3, delta].wait_recv()
        s["b1"][delta] = s["gb"][delta, zrows(0), :] + s["rbp"][3, delta].astype(f32) + s["rbm"][3, delta].astype(f32)
    by = []
    for r in (2, 1, 3):
        s["sy"][r] = s["b1"][r].astype(bf16)
        by.append(send(s["sy"].at[r], s["ry"].at[r], yr[r]))

    for cp in le_cp:
        cp.wait_recv()
    normalise(s["leb"], s["lhat"])
    kcol = to_col(kf, K)
    l_cp = share(s["ls"], exp_total(s["lhat"]), own_product(s["lhat"], kcol.astype(jnp.int32)))

    ref_row = loss_row(s["rs"], r_cp)
    loss_out[...] = jnp.zeros((8, 2 * E), f32)
    loss_out[0:1, 0:E] = ref_row
    learn_row = loss_row(s["ls"], l_cp)
    picked = jnp.sum(jnp.where(iota((K, E), 1).astype(f32) == kcol, ref_row, 0.0), axis=1, keepdims=True)
    loss_out[0:1, E : 2 * E] = learn_row - to_row(picked, E)

    other = pl.ds(pl.multiple_of((1 - c) * (CH // 2), 8), CH // 2)
    own = pl.ds(pl.multiple_of(c * (CH // 2), 8), CH // 2)
    for cp in by:
        cp.wait_recv()
    s["res"][:, CA:FH] = s["b1"][0] + sum(s["ry"][r].astype(f32) for r in range(1, NY))
    fin = [send(s["res"].at[other, pl.ds(CA, FH - CA)], s["fin"].at[:, pl.ds(CA, FH - CA)], sib)]
    for cp in az:
        cp.wait_recv()
    s["res"][:, 0:CA] = s["a1"][zrows(0), :] + sum(s["rz"][r].astype(f32) for r in range(1, NZ))
    fin.append(send(s["res"].at[other, pl.ds(0, CA)], s["fin"].at[:, pl.ds(0, CA)], sib))
    mine = s["res"][own, :]
    wait_both(fin)
    theirs = s["fin"][...]
    grad_out[:, 0:FH] = jnp.where(c == 0, mine, theirs)
    grad_out[:, FH : 2 * FH] = jnp.where(c == 0, theirs, mine)

    for cp in copies:
        cp.wait_send()


def results(losses, grad, ref_out, learn_out, grad_out):
    ref_out[...] = losses[0:1, 0:E]
    learn_out[...] = losses[0:1, E : E + K]
    grad_out[...] = grad[0:22, :]


def per_device(patches, text, ref_proj, w_up, w_down, kept_index, dest, cotan):
    vmem = pl.BlockSpec(memory_space=pltpu.VMEM)
    hbm = pl.BlockSpec(memory_space=pl.ANY)
    scratch = [pltpu.VMEM(shape, dtype) for shape, dtype in SCRATCH.values()]
    scratch += [
        pltpu.SemaphoreType.DMA((N_COPIES,)),
        pltpu.SemaphoreType.DMA((N_COPIES,)),
        pltpu.SemaphoreType.DMA((N_LOCAL,)),
    ]
    losses, grad = pl.pallas_call(
        kernel,
        out_shape=(jax.ShapeDtypeStruct((8, 2 * E), f32), jax.ShapeDtypeStruct((CH // 2, 2 * FH), f32)),
        in_specs=[vmem] * 5 + [hbm] * 3,
        out_specs=(vmem, vmem),
        scratch_shapes=scratch,
        compiler_params=pltpu.CompilerParams(
            collective_id=0, has_side_effects=True, vmem_limit_bytes=56 * 1024 * 1024
        ),
        name="contrastive_step",
    )(patches.T, text, cotan.T, kept_index.reshape(1, K), dest.reshape(1, K), ref_proj, w_up, w_down)
    ref_loss, learnability, grad_up = pl.pallas_call(
        results,
        out_shape=(
            jax.ShapeDtypeStruct((1, E), f32),
            jax.ShapeDtypeStruct((1, K), f32),
            jax.ShapeDtypeStruct((22, 2 * FH), f32),
        ),
        in_specs=[vmem] * 2,
        out_specs=(vmem,) * 3,
        name="results",
    )(losses, grad)
    return (ref_loss.reshape(E), learnability.reshape(K), grad_up)


def solution(mesh):
    in_specs = (
        P("sel", "mdl"),
        P("sel", "mdl"),
        P(None, "mdl"),
        P(None, "mdl"),
        P("mdl", None),
        P("sel"),
        P("sel"),
        P("sel", "mdl"),
    )
    out_specs = (P("sel"), P("sel"), P("sel", "mdl"))
    return jax.shard_map(
        per_device, mesh=mesh, in_specs=in_specs, out_specs=out_specs, check_vma=False
    )
```

time: 91.2 us -> 74.3 us (0.81); the launches traced: 89.4 us -> 74.2 us
  local copies, waits for them, and re-layouts: 7.83 us -> 0 us
  Pallas kernels: 80.9 us -> 73.5 us
    unnamed x5 -> x0, local copies, waits for them, and re-layouts: 7.83 us -> none
    pallas_call x1 -> x2, Pallas kernels: 80.9 us -> 73.5 us  [the longest x1 71.9 us: per_device(): pl.pallas_call(kernel, out_shape=(jax.ShapeDtypeStruct((8, 2 * E), f32),...]
where the time goes in v3:
time: 74.3 us; the launch traced here: 74.2 us
  Pallas kernels  73.5 us (99%)
    pallas_call x1, Pallas kernels, per_device(): pl.pallas_call(kernel, out_shape=(jax.ShapeDtypeStruct((8, 2 * E), f32),...  71.9 us
    pallas_call x1, Pallas kernels, per_device(): pl.pallas_call(results, out_shape=(jax.ShapeDtypeStruct((1, E), f32), jax...  1.6 us

profile of v3, /device:TPU:25, one launch (start us, length us, event | category | flops | bytes accessed | tf_op | source)
XLA Modules:
  0.0 74.2 jit_solution(2563263731392918384)
XLA Ops:
  0.6 71.9 %contrastive_step.1 = (f32[8,256]{1,0:T(8,128)}, f32[24,1536]{1,0:T(8,128)}) custom-call(bf16[352,768]{1,0:T(8,128)(2,1)} %bitcast.6, bf16[128,256]{1,0:T(8,128)(2,1)} %text.1, bf16[352,384]{1,0:T(8,128)(2,1)} %bitcast.7, s32[1,64]{1,0:T(1,128)} %bitcast.8, s32[1,64]{1,0:T(1,128)} %bitcast.9, bf16[1408,256]{1,0:T(8,128)(2,1)} %proj_hbm.1, ...), custom_call_target="tpu_custom_call" | custom-call | tf_op jit(solution)/shard_map/contrastive_step/pallas_call | solution.py:589
  72.6 1.6 %results.1 = (f32[1,128]{1,0:T(1,128)}, f32[1,64]{1,0:T(1,128)}, f32[22,1536]{1,0:T(8,128)}) custom-call(f32[8,256]{1,0:T(8,128)} %get-tuple-element.8.losses, f32[24,1536]{1,0:T(8,128)} %get-tuple-element.9.grad), custom_call_target="tpu_custom_call" | custom-call | tf_op jit(solution)/shard_map/results/pallas_call | solution.py:600

commit v4 on v3

--- a/solution.py
+++ b/solution.py
@@ -26,7 +26,7 @@
 GROUPS = [(0, 1), (1, 2), (3, 2), (5, 2), (7, 1)]
 
 N_COPIES = 150
-N_LOCAL = 3
+N_LOCAL = 5
 
 
 def dot(a, b):
@@ -72,6 +72,7 @@
 
 
 SCRATCH = dict(
+    pat=((DP, E * PATCH), bf16),
     proj=((D, EP), bf16),
     wup=((D, FH), bf16),
     wdn=((FH, D), bf16),
@@ -90,8 +91,8 @@
     hy=((NY, 8, 128), f32),
     mb=((2, NX, K, DP), f32),
     mr=((NX, K, DP), f32),
-    mx=((NX, K, DP), f32),
-    mxr=((NX, K, DP), f32),
+    mx=((NX, K, DP), bf16),
+    mxr=((NX, K, DP), bf16),
     lpb=((NX, K, DP), bf16),
     leb=((NX, K, EP), bf16),
     lhat=((K, EMB), bf16),
@@ -121,7 +122,7 @@
 )
 
 
-def kernel(patches, text, cotan, kidx, dest, proj_hbm, wup_hbm, wdn_hbm, loss_out, grad_out, *scratch):
+def kernel(patches_hbm, text, cotan_hbm, kidx, dest, proj_hbm, wup_hbm, wdn_hbm, loss_out, grad_out, *scratch):
     names = list(SCRATCH)
     s = dict(zip(names, scratch[: len(names)]))
     send_sem, recv_sem, local_sem = scratch[len(names) :]
@@ -164,6 +165,13 @@
     def xblock(slot):
         return pl.ds(pl.multiple_of(lax.rem(x + NX - slot, NX) * DP, 32), DP)
 
+    patches = s["pat"]
+    rows_in = [
+        pltpu.make_async_copy(patches_hbm, patches, local_sem.at[3]),
+        pltpu.make_async_copy(cotan_hbm, s["cot"].at[0, 0], local_sem.at[4]),
+    ]
+    for load in rows_in:
+        load.start()
     barrier = pltpu.get_barrier_semaphore()
     for p in partners:
         pl.semaphore_signal(barrier, inc=1, device_id=p, device_id_type=MESH)
@@ -181,10 +189,12 @@
     line = iota((R, 1), 0).astype(f32)
     entry = spread(iota((1, K), 1).astype(f32))
     want = (PATCH * krow + (line - PATCH * entry)).astype(jnp.int32)
-    s["tok"][0, 0] = dot_nt(patches[...], one_hot(iota((R, E * PATCH), 1) == want)).astype(bf16)
-    s["cot"][0, 0] = cotan[...]
+    pick = one_hot(iota((R, E * PATCH), 1) == want)
     s["dst"][0] = jnp.zeros((8, 128), f32)
     s["dst"][0, 0:1, 0:K] = dest[...].astype(f32)
+    for load in rows_in:
+        load.wait()
+    s["tok"][0, 0] = dot_nt(patches[...], pick).astype(bf16)
 
     pl.semaphore_wait(barrier, len(partners))
 
@@ -365,7 +375,7 @@
 
     m_c.wait_recv()
     for slot in range(NX):
-        s["mx"][slot] = s["mb"][0, slot] + s["mr"][slot]
+        s["mx"][slot] = (s["mb"][0, slot] + s["mr"][slot]).astype(bf16)
     mx_cp = [send(s["mx"].at[NX - r], s["mxr"].at[r], xr[r]) for r in range(1, NX)]
 
     wait_both(cotc)
@@ -440,20 +450,6 @@
     as2.append(send(s["sam"].at[1, pl.ds(0, hg)], s["ram"].at[1, pl.ds(0, hg)], ym))
     ga(0)
 
-    txt_c = [send(s["txt"].at[0], s["txt"].at[NY], sib)]
-    wait_both(ys[3])
-    ys2.append(send(yg(3, 3), yg(2, 3), ym))
-    wait_both(ys[4])
-    ys2.append(send(yg(1, 4), yg(2, 4), yp))
-    txt_c += [send(s["txt"].at[i], s["txt"].at[NY + i], sib) for i in (1, 3)]
-
-    for cp in mx_cp:
-        cp.wait_recv()
-    tok_mean = dot_nt(one_hot(pool_mask(K, R)), s["tok"][0, 0]) * (1.0 / PATCH)
-    mixed = s["mx"][0] + s["mxr"][1] + s["mxr"][2] + s["mxr"][3]
-    s["lpb"][0] = (tok_mean + mixed).astype(bf16)
-    lp_cp = [send(s["lpb"].at[0], s["lpb"].at[r], xr[r]) for r in range(1, NX)]
-
     b_step(2)
 
     loads[2].wait()
@@ -471,11 +467,18 @@
 
     b_step(3)
 
-    for cp in lp_cp:
-        cp.wait_recv()
-    emb = sum(dot(s["lpb"][slot], s["proj"][xblock(slot), :]) for slot in range(NX))
-    s["leb"][0] = emb.astype(bf16)
-    le_cp = [send(s["leb"].at[0], s["leb"].at[r], xr[r]) for r in range(1, NX)]
+    wait_both(ys[3])
+    ys2.append(send(yg(3, 3), yg(2, 3), ym))
+    wait_both(ys[4])
+    ys2.append(send(yg(1, 4), yg(2, 4), yp))
+    txt_c = [send(s["txt"].at[i], s["txt"].at[NY + i], sib) for i in (0, 1, 3)]
+
+    for cp in mx_cp:
+        cp.wait_recv()
+    tok_mean = dot_nt(one_hot(pool_mask(K, R)), s["tok"][0, 0]) * (1.0 / PATCH)
+    mixed = s["mb"][0, 0] + s["mr"][0] + sum(s["mxr"][r].astype(f32) for r in range(1, NX))
+    s["lpb"][0] = (tok_mean + mixed).astype(bf16)
+    lp_cp = [send(s["lpb"].at[0], s["lpb"].at[r], xr[r]) for r in range(1, NX)]
 
     def normalise(blocks, out):
         v = [blocks[slot].astype(f32) for slot in range(NX)]
@@ -512,12 +515,6 @@
     for cp in eb_cp:
         cp.wait_recv()
     normalise(s["eb"], s["ihat"])
-    for cp in ys2:
-        cp.wait_recv()
-    txt_c.append(send(s["txt"].at[2], s["txt"].at[NY + 2], sib))
-    for cp in txt_c:
-        cp.wait_recv()
-    r_cp = share(s["rs"], exp_total(s["ihat"]), own_product(s["ihat"], iota((E, 1), 0)))
 
     b_step(4)
 
@@ -528,6 +525,12 @@
     for r in (4, 3, 5, 2, 6, 1, 7):
         s["sz"][r] = s["a1"][zrows(r), :].astype(bf16)
         az.append(send(s["sz"].at[r], s["rz"].at[r], zr[r]))
+
+    for cp in lp_cp:
+        cp.wait_recv()
+    emb = sum(dot(s["lpb"][slot], s["proj"][xblock(slot), :]) for slot in range(NX))
+    s["leb"][0] = emb.astype(bf16)
+    le_cp = [send(s["leb"].at[0], s["leb"].at[r], xr[r]) for r in range(1, NX)]
 
     for delta in range(NY):
         b_cp[True, 3, delta].wait_recv()
@@ -537,6 +540,13 @@
     for r in (2, 1, 3):
         s["sy"][r] = s["b1"][r].astype(bf16)
         by.append(send(s["sy"].at[r], s["ry"].at[r], yr[r]))
+
+    for cp in ys2:
+        cp.wait_recv()
+    txt_c.append(send(s["txt"].at[2], s["txt"].at[NY + 2], sib))
+    for cp in txt_c:
+        cp.wait_recv()
+    r_cp = share(s["rs"], exp_total(s["ihat"]), own_product(s["ihat"], iota((E, 1), 0)))
 
     for cp in le_cp:
         cp.wait_recv()
@@ -589,7 +599,7 @@
     losses, grad = pl.pallas_call(
         kernel,
         out_shape=(jax.ShapeDtypeStruct((8, 2 * E), f32), jax.ShapeDtypeStruct((CH // 2, 2 * FH), f32)),
-        in_specs=[vmem] * 5 + [hbm] * 3,
+        in_specs=[hbm, vmem, hbm, vmem, vmem] + [hbm] * 3,
         out_specs=(vmem, vmem),
         scratch_shapes=scratch,
         compiler_params=pltpu.CompilerParams(

time: 74.3 us -> 73 us (0.983)
  Pallas kernels: 73.5 us -> 72 us
    pallas_call x1, Pallas kernels: 71.9 us -> 70.3 us  [per_device(): pl.pallas_call(kernel, out_shape=(jax.ShapeDtypeStruct((8, 2 * E), f32),...]
where the time goes in v4:
time: 73 us; the launch traced here: 72.6 us
  Pallas kernels  72 us (99%)
    pallas_call x1, Pallas kernels, per_device(): pl.pallas_call(kernel, out_shape=(jax.ShapeDtypeStruct((8, 2 * E), f32),...  70.3 us
    pallas_call x1, Pallas kernels, per_device(): pl.pallas_call(results, out_shape=(jax.ShapeDtypeStruct((1, E), f32), jax...  1.6 us

profile of v4, /device:TPU:25, one launch (start us, length us, event | category | flops | bytes accessed | tf_op | source)
XLA Modules:
  0.0 72.6 jit_solution(4689153159100199545)
XLA Ops:
  0.6 70.3 %contrastive_step.1 = (f32[8,256]{1,0:T(8,128)}, f32[24,1536]{1,0:T(8,128)}) custom-call(bf16[352,768]{1,0:T(8,128)(2,1)} %bitcast.6, bf16[128,256]{1,0:T(8,128)(2,1)} %text.1, bf16[352,384]{1,0:T(8,128)(2,1)} %bitcast.7, s32[1,64]{1,0:T(1,128)} %bitcast.8, s32[1,64]{1,0:T(1,128)} %bitcast.9, bf16[1408,256]{1,0:T(8,128)(2,1)} %proj_hbm.1, ...), custom_call_target="tpu_custom_call" | custom-call | tf_op jit(solution)/shard_map/contrastive_step/pallas_call | solution.py:599
  71.0 1.6 %results.1 = (f32[1,128]{1,0:T(1,128)}, f32[1,64]{1,0:T(1,128)}, f32[22,1536]{1,0:T(8,128)}) custom-call(f32[8,256]{1,0:T(8,128)} %get-tuple-element.8.losses, f32[24,1536]{1,0:T(8,128)} %get-tuple-element.9.grad), custom_call_target="tpu_custom_call" | custom-call | tf_op jit(solution)/shard_map/results/pallas_call | solution.py:610

commit v5 on v4

--- a/solution.py
+++ b/solution.py
@@ -334,7 +334,6 @@
         lax.fori_loop(0, R // 32, act_step, 0)
 
     cot2 = ring_forward(s["cot"], cot1[0])
-    pb_cp = [send(s["pb"].at[0], s["pb"].at[r], xr[r]) for r in range(1, NX)]
 
     pooled_h = dot(one_hot(pool_mask(2 * K, 2 * R)), s["hid"][...]) * (1.0 / PATCH)
     pooled_h = pooled_h.astype(bf16)
@@ -376,7 +375,6 @@
     m_c.wait_recv()
     for slot in range(NX):
         s["mx"][slot] = (s["mb"][0, slot] + s["mr"][slot]).astype(bf16)
-    mx_cp = [send(s["mx"].at[NX - r], s["mxr"].at[r], xr[r]) for r in range(1, NX)]
 
     wait_both(cotc)
     back(1, 1)
@@ -391,6 +389,8 @@
 
     wait_both(cot2)
     cotc2 = to_core(s["cot"], 2)
+    mx_cp = [send(s["mx"].at[NX - r], s["mxr"].at[r], xr[r]) for r in range(1, NX)]
+    pb_cp = [send(s["pb"].at[0], s["pb"].at[r], xr[r]) for r in range(1, NX)]
     back(0, 2)
     z_wait(zs4)
     ys.append(y_first(4))

time: 73 us -> 72.2 us (0.989)
  no operation moved by 1% of the time
where the time goes in v5:
time: 72.2 us; the launch traced here: 72 us
  Pallas kernels  71.4 us (99%)
    pallas_call x1, Pallas kernels, per_device(): pl.pallas_call(kernel, out_shape=(jax.ShapeDtypeStruct((8, 2 * E), f32),...  69.8 us
    pallas_call x1, Pallas kernels, per_device(): pl.pallas_call(results, out_shape=(jax.ShapeDtypeStruct((1, E), f32), jax...  1.6 us

profile of v5, /device:TPU:25, one launch (start us, length us, event | category | flops | bytes accessed | tf_op | source)
XLA Modules:
  0.0 72.0 jit_solution(10366291478310278571)
XLA Ops:
  0.6 69.8 %contrastive_step.1 = (f32[8,256]{1,0:T(8,128)}, f32[24,1536]{1,0:T(8,128)}) custom-call(bf16[352,768]{1,0:T(8,128)(2,1)} %bitcast.6, bf16[128,256]{1,0:T(8,128)(2,1)} %text.1, bf16[352,384]{1,0:T(8,128)(2,1)} %bitcast.7, s32[1,64]{1,0:T(1,128)} %bitcast.8, s32[1,64]{1,0:T(1,128)} %bitcast.9, bf16[1408,256]{1,0:T(8,128)(2,1)} %proj_hbm.1, ...), custom_call_target="tpu_custom_call" | custom-call | tf_op jit(solution)/shard_map/contrastive_step/pallas_call | solution.py:599
  70.4 1.6 %results.1 = (f32[1,128]{1,0:T(1,128)}, f32[1,64]{1,0:T(1,128)}, f32[22,1536]{1,0:T(8,128)}) custom-call(f32[8,256]{1,0:T(8,128)} %get-tuple-element.8.losses, f32[24,1536]{1,0:T(8,128)} %get-tuple-element.9.grad), custom_call_target="tpu_custom_call" | custom-call | tf_op jit(solution)/shard_map/results/pallas_call | solution.py:610
